TPU v7x, 1024 devices: a whole 4x8x16 slice. The times are simulated.
1024 devices in a mesh: group: 32 (over x, y), dom: 32 (over z, core).
Axes of the slice: x: 4, y: 8, z: 16, core: 2. Of those that a mesh axis runs over, the one named last changes fastest.
Arguments:
- modal_state: float32 [1024, 56, 9, 128], P(('group', 'dom')), may hold values from -6 to 6
- geometry: float32 [1024, 3, 128], P(('group', 'dom')), may hold values from 0.5 to 2
- material: int32 [1024, 128], P(('group', 'dom')), may hold values from 0 to 7
- star_table: float32 [8, 3, 9, 9], replicated, may hold values from -0.75 to 0.75
- flux_table: float32 [8, 2, 9, 9], replicated, may hold values from -0.625 to 0.625
- cohesion: float32 [8], replicated, may hold values from 0.5 to 4
- stiffness: float32 [3, 56, 56], replicated, may hold values from -0.75 to 0.75
- face_project: float32 [4, 21, 56], replicated, may hold values from -0.75 to 0.75
- face_lift: float32 [4, 56, 21], replicated, may hold values from -1.25 to 1.25
- reorient: float32 [3, 21, 21], replicated, may hold values from -1.25 to 1.25
- neighbour_face: int32 [2, 1024, 512], P(None, ('group', 'dom')), may hold values from 0 to 767, as said below
- send_faces: int32 [2, 1024, 4, 64], P(None, ('group', 'dom')), may hold values from 0 to 511
- orientation: int32 [2, 1024, 512], P(None, ('group', 'dom')), may hold values from 0 to 2
- leaving_slots: int32 [1024, 32], P(('group', 'dom')), may hold values from 0 to 127, as said below
- leaving_owner: int32 [1024, 32], P('group'), may hold values from 0 to 31, as said below
Outputs:
- final_state: float32 [1024, 56, 9, 128], P(('group', 'dom'))
Inputs may be any that keep to these rules, and one draw needn't show every extreme that they name: `neighbour_face`: entries below 512 name a local trace; entry 512 + m names received trace m; every received trace is named exactly once in each phase and device. `leaving_slots`: each device's entries are distinct and increasing. `leaving_owner`: every device receives exactly 32 elements; at most 2 go from one device to any one device, and in every group some pair reaches 2.
All inputs are finite; a program needn't handle non-finite values.
Results may differ from a plain program's by a relative error of at most 0.0003.
Values sent between devices are 32-bit elements; how exact they have to be, the bound alone decides.
No kernel may reach another device: no remote copies, remote signals or barrier semaphores. Data moves between devices by JAX's collectives and lax.ppermute only.
A program may use at most 128 MiB of HBM per device.

v0:
```python
import functools

import jax
import jax.numpy as jnp
from jax import lax
from jax.experimental import pallas as pl
from jax.experimental.pallas import tpu as pltpu
from jax.sharding import PartitionSpec as P

TAYLOR = 6
FIELDS = 9
LANES = 128
FACE_PAD = 24
TRACE_ROWS = FIELDS * FACE_PAD
MSG_ROWS = 112
STAR_ROWS = 243
OPS_ROWS = 408
VALUES = 512

highest = lax.Precision.HIGHEST
friction_coef = 0.6
relax_share = 0.5
f32 = jnp.float32
bf16 = jnp.bfloat16


def halves(x):
    hi = x.astype(bf16)
    return hi, (x - hi.astype(f32)).astype(bf16)


def left_matrix(a):
    hi, lo = halves(a)
    both = jnp.concatenate([hi.astype(f32), lo.astype(f32)], axis=0).astype(bf16)
    return both, hi


def mm(left, x):
    both, hi = left
    x_hi, x_lo = halves(x)
    rows = hi.shape[0]
    first = jnp.dot(both, x_hi, preferred_element_type=f32)
    return first[:rows] + (first[rows:] + jnp.dot(hi, x_lo, preferred_element_type=f32))


def lane_gather(x, lane):
    return jnp.take_along_axis(x, jnp.broadcast_to(lane, x.shape), axis=1, mode="promise_in_bounds")


def block(f):
    return slice(f * LANES, (f + 1) * LANES)


def spread_rows(ops_ref, first, count, wide_ref):
    for r in range(count):
        wide_ref[r] = jnp.broadcast_to(ops_ref[first + r : first + r + 1, :], (8, LANES))


def mix(load, wide_ref, start, outs):
    accs = [None] * len(outs)
    for f in range(FIELDS):
        value = load(f)
        rows = value.shape[0]
        value = value.reshape(rows // 8, 8, LANES)
        for t, g in enumerate(outs):
            part = value * wide_ref[start + f * FIELDS + g][None]
            accs[t] = part if accs[t] is None else accs[t] + part
    return [a.reshape(-1, LANES) for a in accs]


GROUPS_OF_FIELDS = ((0, 1, 2), (3, 4, 5), (6, 7, 8))


def star_mixed(src_ref, wide_ref, outs):
    load = lambda f: src_ref[:, block(f)]
    parts = []
    for d in range(3):
        parts.append(jnp.concatenate(mix(load, wide_ref, d * 81, outs), axis=1))
    return jnp.concatenate(parts, axis=0)


def first_half_body(place, refs):
    if place:
        (state_ref, recv_ref, qmap_ref, desc_ref, table_ref, send_ref, stiff_ref, project_ref,
         integral_ref, trace_ref, m0, m1, m2, m3, ops_ref, placed_ref,
         wide_ref, deriv_ref) = refs
    else:
        (state_ref, desc_ref, table_ref, send_ref, stiff_ref, project_ref,
         integral_ref, trace_ref, m0, m1, m2, m3, ops_ref, desc_out_ref,
         wide_ref, deriv_ref) = refs
    modes = stiff_ref.shape[0]

    desc = desc_ref[...]
    if place:
        qmap = qmap_ref[...]
        arrives = qmap >= 0
        lane = jnp.maximum(qmap, 0)
        moved = []
        for b in range(4):
            got = recv_ref[pl.ds(b, 64, stride=4), :]
            got = jnp.concatenate([got, got], axis=0)
            moved.append(lane_gather(jnp.transpose(got, (1, 0)), lane))
        moved = jnp.concatenate(moved, axis=0)
        for f in range(FIELDS):
            new = jnp.where(arrives, moved[f * modes : (f + 1) * modes], state_ref[:, block(f)])
            placed_ref[:, block(f)] = new
        desc = jnp.where(arrives, moved[FIELDS * modes :], desc)
        state_now = placed_ref
    else:
        desc_out_ref[...] = desc
        for f in range(FIELDS):
            integral_ref[:, block(f)] = state_ref[f]
        state_now = integral_ref

    kinds = lax.broadcasted_iota(jnp.int32, (8, LANES), 0).astype(f32)
    hot = (jnp.broadcast_to(desc[3:4], (8, LANES)) == kinds).astype(f32)
    rows = jnp.dot(table_ref[...], hot, precision=highest, preferred_element_type=f32)
    row_at = lax.broadcasted_iota(jnp.int32, (OPS_ROWS, LANES), 0)
    scale = jnp.where(
        row_at < 81,
        desc[0:1],
        jnp.where(row_at < 162, desc[1:2], jnp.where(row_at < STAR_ROWS, desc[2:3], 1.0)),
    )
    ops_ref[...] = rows * scale
    spread_rows(ops_ref, 0, STAR_ROWS, wide_ref)

    stiff = left_matrix(-stiff_ref[...])
    deriv_ref[0] = state_now[...]
    if place:
        integral_ref[...] = state_now[...]

    def degree(j, carry):
        coef = carry
        now = deriv_ref.at[lax.rem(j, 2)]
        later = deriv_ref.at[lax.rem(j + 1, 2)]
        for outs in GROUPS_OF_FIELDS:
            new = mm(stiff, star_mixed(now, wide_ref, outs))
            lanes = slice(outs[0] * LANES, (outs[-1] + 1) * LANES)
            later[:, lanes] = new
            integral_ref[:, lanes] = integral_ref[:, lanes] + new * coef
        return coef / (j + 3).astype(f32)

    lax.fori_loop(0, TAYLOR - 1, degree, jnp.float32(0.5))

    project = left_matrix(project_ref[...])
    for outs in GROUPS_OF_FIELDS:
        lanes = slice(outs[0] * LANES, (outs[-1] + 1) * LANES)
        traced = mm(project, integral_ref[:, lanes])
        for t, f in enumerate(outs):
            for i in range(4):
                trace_ref[i, f * FACE_PAD : (f + 1) * FACE_PAD, :] = traced[
                    i * FACE_PAD : (i + 1) * FACE_PAD, block(t)
                ]

    low = lax.broadcasted_iota(jnp.int32, (8, LANES), 1) < 64
    for c, msg_ref in enumerate((m0, m1, m2, m3)):
        index = jnp.broadcast_to(send_ref[c : c + 1, :], (8, LANES))
        lane, face = index & 127, index >> 7
        for r in range(MSG_ROWS // 8):
            out = None
            for i in range(4):
                got = lane_gather(trace_ref[i, r * 8 : r * 8 + 8, :], lane)
                high_row = r * 8 + MSG_ROWS
                if high_row < TRACE_ROWS:
                    other = lane_gather(trace_ref[i, high_row : high_row + 8, :], lane)
                    got = jnp.where(low, got, other)
                out = got if out is None else jnp.where(face == i, got, out)
            msg_ref[r * 8 : r * 8 + 8, :] = out


def middle_body(refs):
    (state_ref, integral_ref, trace_ref, ops_ref, near_ref, volume_ref, own_ref,
     partial_ref, local_ref, wide_ref) = refs
    spread_rows(ops_ref, 0, STAR_ROWS + 81, wide_ref)
    volume = left_matrix(volume_ref[...])
    own = left_matrix(own_ref[...])
    for outs in GROUPS_OF_FIELDS:
        lanes = slice(outs[0] * LANES, (outs[-1] + 1) * LANES)
        load = lambda f: integral_ref[:, block(f)]
        added = mm(volume, star_mixed(integral_ref, wide_ref, outs))
        flux = mm(own, jnp.concatenate(mix(load, wide_ref, STAR_ROWS, outs), axis=1))
        if len(state_ref.shape) == 3:
            before = jnp.concatenate([state_ref[g] for g in outs], axis=1)
        else:
            before = state_ref[:, lanes]
        partial_ref[:, lanes] = before + added - flux
    for i in range(4):
        index = jnp.broadcast_to(near_ref[i : i + 1, :], (8, LANES))
        lane, source = index & 127, index >> 7
        for r in range(TRACE_ROWS // 8):
            rows = slice(r * 8, r * 8 + 8)
            out = None
            for j in range(4):
                got = lane_gather(trace_ref[j, rows, :], lane)
                out = got if out is None else jnp.where(source == j, got, out)
            local_ref[i, rows, :] = out


def last_half_body(pack, refs):
    if pack:
        (partial_ref, local_ref, m0, m1, m2, m3, ops_ref, near_ref, orient_ref, lift_ref,
         desc_ref, src_ref, out_ref, packed_ref, wide_ref, both_ref, turned_ref, sum_ref) = refs
    else:
        (partial_ref, local_ref, m0, m1, m2, m3, ops_ref, near_ref, orient_ref, lift_ref,
         out_ref, wide_ref, both_ref, turned_ref, sum_ref) = refs
    modes = lift_ref.shape[0]
    spread_rows(ops_ref, STAR_ROWS + 81, 81, wide_ref)

    low = lax.broadcasted_iota(jnp.int32, (MSG_ROWS, LANES), 1) < 64
    rest = TRACE_ROWS - MSG_ROWS
    for k, (a, b) in enumerate(((m0, m1), (m2, m3))):
        first, second = a[...], b[...]
        both_ref[k, 0:MSG_ROWS, :] = jnp.where(low, first, pltpu.roll(second, 64, 1))
        upper = jnp.where(low, pltpu.roll(first, 64, 1), second)
        both_ref[k, MSG_ROWS:TRACE_ROWS, :] = upper[:rest]

    for i in range(4):
        index = jnp.broadcast_to(near_ref[i : i + 1, :], (8, LANES))
        lane, source = index & 127, index >> 7
        for r in range(TRACE_ROWS // 8):
            rows = slice(r * 8, r * 8 + 8)
            out = local_ref[i, rows, :]
            for k in range(2):
                out = jnp.where(source == 4 + k, lane_gather(both_ref[k, rows, :], lane), out)
            turned_ref[i, rows, :] = out

    lift = left_matrix(lift_ref[...])
    for outs in GROUPS_OF_FIELDS:
        lanes = slice(outs[0] * LANES, (outs[-1] + 1) * LANES)
        pieces = []
        for i in range(4):
            load = lambda f: turned_ref[i, f * FACE_PAD : (f + 1) * FACE_PAD, :]
            mixed = mix(load, wide_ref, 0, outs)
            orient = jnp.broadcast_to(orient_ref[i : i + 1, :], (FACE_PAD, LANES))
            for h in range(3):
                pieces.append(
                    jnp.concatenate([jnp.where(orient == h, m, 0.0) for m in mixed], axis=1)
                )
        flux = mm(lift, jnp.concatenate(pieces, axis=0))
        wide_out = partial_ref[:, lanes] - flux
        for t, g in enumerate(outs):
            sum_ref[:, block(g)] = wide_out[:, block(t)]

    zero = [sum_ref[0:1, block(f)] for f in range(6)]
    pressure_zero = -(zero[0] + zero[1] + zero[2]) / 3.0
    second = 0.5 * sum((zero[f] + pressure_zero) * (zero[f] + pressure_zero) for f in range(3))
    second = second + sum(zero[f] * zero[f] for f in range(3, 6))
    shear_mag = jnp.sqrt(second)
    yield_row = ops_ref[405:406, :]
    yield_stress = yield_row + friction_coef * jnp.maximum(pressure_zero, 0.0)
    factor = 1.0 - relax_share * jnp.maximum(
        0.0, 1.0 - yield_stress / jnp.maximum(shear_mag, yield_stress)
    )
    normals = [sum_ref[:, block(f)] for f in range(3)]
    pressure = -(normals[0] + normals[1] + normals[2]) / 3.0
    fields = [-pressure + factor * (n + pressure) for n in normals]
    fields += [factor * sum_ref[:, block(f)] for f in range(3, 6)]
    fields += [sum_ref[:, block(f)] for f in range(6, FIELDS)]
    if not pack:
        for f in range(FIELDS):
            out_ref[f] = fields[f]
        return
    for f in range(FIELDS):
        out_ref[:, block(f)] = fields[f]
    values = jnp.concatenate(fields + [desc_ref[...]], axis=0)
    leaving = lane_gather(values, src_ref[...])
    for b in range(4):
        turned = jnp.transpose(leaving[b * LANES : (b + 1) * LANES], (1, 0))
        packed_ref[pl.ds(b, 64, stride=4), :] = turned[:64]


def call(body, outs, scratch, *args):
    return pl.pallas_call(
        lambda *refs: body(refs),
        out_shape=[jax.ShapeDtypeStruct(s, f32) for s in outs],
        in_specs=[pl.BlockSpec(memory_space=pltpu.VMEM)] * len(args),
        out_specs=[pl.BlockSpec(memory_space=pltpu.VMEM)] * len(outs),
        scratch_shapes=[pltpu.VMEM(s, f32) for s in scratch],
        compiler_params=pltpu.CompilerParams(vmem_limit_bytes=48 << 20),
    )(*args)


def exchange(messages):
    out = []
    for axis, (lower, higher) in (("group", messages[:2]), ("dom", messages[2:])):
        size = lax.axis_size(axis)
        up = [(i, (i + 1) % size) for i in range(size)]
        down = [(j, i) for i, j in up]
        out += [lax.ppermute(higher, axis, up), lax.ppermute(lower, axis, down)]
    return out


def migration_maps(own_slots, leaving_owner, elem_count):
    dom_count = lax.axis_size("dom")
    my_dom = lax.axis_index("dom")
    leave_count = own_slots.shape[0]
    capacity = 2 * leave_count // dom_count
    slot_total = capacity * dom_count
    own_owner = lax.dynamic_index_in_dim(leaving_owner, my_dom, 0, keepdims=False)
    order = jnp.arange(leave_count, dtype=jnp.int32)
    slot_ids = jnp.arange(slot_total, dtype=jnp.int32)
    same = (own_owner[None, :] == own_owner[:, None]) & (order[None, :] < order[:, None])
    send_slot = own_owner * capacity + jnp.sum(same.astype(jnp.int32), axis=1)
    source_lane = jnp.sum(
        jnp.where(send_slot[None, :] == slot_ids[:, None], own_slots[None, :], 0), axis=1
    )
    arrivals = jnp.sum((leaving_owner == my_dom).astype(jnp.int32), axis=1)
    doms = jnp.arange(dom_count, dtype=jnp.int32)
    sender, within = slot_ids // capacity, slot_ids % capacity
    ahead = jnp.sum(jnp.where(doms[None, :] < sender[:, None], arrivals[None, :], 0), axis=1)
    mine = jnp.sum(jnp.where(doms[None, :] == sender[:, None], arrivals[None, :], 0), axis=1)
    position = jnp.where(within < mine, ahead + within, -1)
    elems = jnp.arange(elem_count, dtype=jnp.int32)
    rank = (
        jnp.sum(jnp.where(own_slots[:, None] == elems[None, :], order[:, None] + 1, 0), axis=0) - 1
    )
    hit = (position[:, None] == rank[None, :]) & (rank[None, :] >= 0)
    arriving = jnp.sum(jnp.where(hit, slot_ids[:, None] + 1, 0), axis=0) - 1
    source_lane = jnp.concatenate([source_lane, source_lane])
    return source_lane[None, :], arriving[None, :]


def shards(
    modal_state,
    geometry,
    material,
    star_table,
    flux_table,
    cohesion,
    stiffness,
    face_project,
    face_lift,
    reorient,
    neighbour_face,
    send_faces,
    orientation,
    leaving_slots,
    leaving_owner,
):
    modes, nfield, elem_count = modal_state.shape[1:]
    face_modes = face_project.shape[1]
    kinds = star_table.shape[0]
    trace_pad = FACE_PAD - face_modes

    state = jnp.transpose(modal_state[0], (1, 0, 2))
    desc = jnp.concatenate(
        [geometry[0], material[0][None].astype(f32), jnp.zeros((4, elem_count), f32)], axis=0
    )
    table = jnp.concatenate(
        [
            star_table.reshape(kinds, -1),
            flux_table.reshape(kinds, -1),
            cohesion[:, None],
            jnp.zeros((kinds, OPS_ROWS - 406), f32),
        ],
        axis=1,
    ).T
    stiff = jnp.transpose(stiffness, (1, 0, 2)).reshape(modes, 3 * modes)
    volume = jnp.transpose(stiffness, (2, 0, 1)).reshape(modes, 3 * modes)
    project = jnp.pad(face_project, ((0, 0), (0, trace_pad), (0, 0))).reshape(4 * FACE_PAD, modes)
    own = jnp.einsum("iml,iln->mn", face_lift, face_project, precision=highest)
    turned = jnp.einsum("iml,hlk->mihk", face_lift, reorient, precision=highest)
    lift = jnp.pad(turned, ((0, 0), (0, 0), (0, 0), (0, trace_pad))).reshape(modes, -1)

    send = jnp.concatenate([send_faces[:, 0], send_faces[:, 0]], axis=2)
    near = neighbour_face[:, 0].reshape(2, 4, elem_count)
    orient = orientation[:, 0].reshape(2, 4, elem_count)
    source_lane, arriving = migration_maps(leaving_slots[0], leaving_owner, elem_count)

    width = nfield * elem_count
    full = (modes, width)
    traces = (4, TRACE_ROWS, LANES)
    msg = (MSG_ROWS, LANES)
    ops_shape = (OPS_ROWS, LANES)
    wide = (STAR_ROWS, 8, LANES)
    wide_more = (STAR_ROWS + 81, 8, LANES)
    wide_flux = (81, 8, LANES)

    def middle(state_now, integral, trace, ops, phase):
        return call(middle_body, [full, traces], [wide_more],
                    state_now, integral, trace, ops, near[phase], volume, own)

    integral, trace, a, b, c, d, ops, desc = call(
        functools.partial(first_half_body, False),
        [full, traces, msg, msg, msg, msg, ops_shape, (8, LANES)],
        [wide, (2,) + full],
        state, desc, table, send[0], stiff, project,
    )
    incoming = exchange([a, b, c, d])
    partial, local = middle(state, integral, trace, ops, 0)
    stepped, packed = call(
        functools.partial(last_half_body, True),
        [full, (256, LANES)],
        [wide_flux, (2,) + traces[1:], traces, full],
        partial, local, *incoming, ops, near[0], orient[0], lift, desc, source_lane,
    )
    moved = lax.all_to_all(packed, "dom", split_axis=0, concat_axis=0, tiled=True)
    integral, trace, a, b, c, d, ops, placed = call(
        functools.partial(first_half_body, True),
        [full, traces, msg, msg, msg, msg, ops_shape, full],
        [wide, (2,) + full],
        stepped, moved, arriving, desc, table, send[1], stiff, project,
    )
    incoming = exchange([a, b, c, d])
    partial, local = middle(placed, integral, trace, ops, 1)
    (final,) = call(
        functools.partial(last_half_body, False),
        [(nfield, modes, elem_count)],
        [wide_flux, (2,) + traces[1:], traces, full],
        partial, local, *incoming, ops, near[1], orient[1], lift,
    )
    return jnp.transpose(final, (1, 0, 2))[None]


def solution(mesh):
    in_specs = (
        P(("group", "dom"), None, None, None),
        P(("group", "dom"), None, None),
        P(("group", "dom"), None),
        P(),
        P(),
        P(),
        P(),
        P(),
        P(),
        P(),
        P(None, ("group", "dom"), None),
        P(None, ("group", "dom"), None, None),
        P(None, ("group", "dom"), None),
        P(("group", "dom"), None),
        P("group", None),
    )
    out_specs = P(("group", "dom"), None, None, None)
    return jax.shard_map(shards, mesh=mesh, in_specs=in_specs, out_specs=out_specs, check_vma=False)
```

profile of v0, /device:TPU:1, one launch (start us, length us, event | category | flops | bytes accessed | tf_op | source)
XLA Modules:
  0.0 91.4 jit_solution(17976391652232583684)
XLA Ops:
  0.0 1.1 %copy.78 = f32[8,3,9,9]{0,3,2,1:T(8,128)S(1)} copy(f32[8,3,9,9]{3,0,2,1:T(8,128)} %param.18) | data formatting | bytes 15552 | tf_op jit(solution)/shard_map/reshape | solution.py:351
  1.2 0.9 copy-done.5
  2.0 0.2 copy.79
  2.2 0.9 copy-done.2
  3.1 0.1 copy.64
  3.2 0.1 copy.66.refs_4_.refs_6_
  3.3 0.7 copy-done.4
  4.0 0.7 copy-done.7
  4.7 0.1 fusion.5
  4.8 0.6 copy-done.10
  5.4 0.1 pad.17.clone
  5.5 0.1 pad.20.clone
  5.6 0.1 maximum_maximum_fusion.refs_1_
  5.6 0.1 maximum_bitcast_fusion.refs_2_.refs_4_
  5.8 0.6 copy-done.1
  6.3 6.4 %shard_map.145 = (f32[56,1152]{1,0:T(8,128)S(1)}, f32[4,216,128]{2,1,0:T(8,128)S(1)}, f32[112,128]{1,0:T(8,128)S(1)}, f32[112,128]{1,0:T(8,128)S(1)}, f32[112,12...) custom-call(f32[9,56,128]{2,1,0:T(8,128)S(1)} %bitcast.59, ...), custom_call_target="tpu_custom_call" | custom-call | tf_op jit(solution)/shard_map/pallas_call | solution.py:273
  12.8 4.0 %collective-permute-start = (f32[112,128]{1,0:T(8,128)S(1)}, f32[112,128]{1,0:T(8,128)S(1)}, u32[]{:S(2)}, u32[]{:S(2)}) collective-permute-start(f32[112,128]{1,0:T(8,128)S(1)} %get-tuple-element.32), channel_id=1, source_target_pairs={{0,32},{32,64},{64,96},{96,128},{128,160},{160,192},{192,224},{224... | collective-permute-start | bytes 172040 | tf_op jit(solution)/shard_map/ppermute | solution.py:289
  16.8 6.0 %collective-permute-start.1 = (f32[112,128]{1,0:T(8,128)S(1)}, f32[112,128]{1,0:T(8,128)S(1)}, u32[]{:S(2)}, u32[]{:S(2)}) collective-permute-start(f32[112,128]{1,0:T(8,128)S(1)} %get-tuple-element.33), channel_id=1, source_target_pairs={{32,0},{64,32},{96,64},{128,96},{160,128},{192,160},{224,192},{256... | collective-permute-start | bytes 172040 | tf_op jit(solution)/shard_map/ppermute | solution.py:289
  22.8 2.9 %collective-permute-start.2 = (f32[112,128]{1,0:T(8,128)S(1)}, f32[112,128]{1,0:T(8,128)S(1)}, u32[]{:S(2)}, u32[]{:S(2)}) collective-permute-start(f32[112,128]{1,0:T(8,128)S(1)} %get-tuple-element.34), channel_id=1, source_target_pairs={{0,1},{1,2},{2,3},{3,4},{4,5},{5,6},{6,7},{7,8},{8,9},{9,10},{10,1... | collective-permute-start | bytes 172040 | tf_op jit(solution)/shard_map/ppermute | solution.py:289
  25.8 10.4 %collective-permute-start.3 = (f32[112,128]{1,0:T(8,128)S(1)}, f32[112,128]{1,0:T(8,128)S(1)}, u32[]{:S(2)}, u32[]{:S(2)}) collective-permute-start(f32[112,128]{1,0:T(8,128)S(1)} %get-tuple-element.35), channel_id=1, source_target_pairs={{1,0},{2,1},{3,2},{4,3},{5,4},{6,5},{7,6},{8,7},{9,8},{10,9},{11,1... | collective-permute-start | bytes 172040 | tf_op jit(solution)/shard_map/ppermute | solution.py:289
  36.2 0.1 copy.69.refs_5_
  36.3 0.7 copy-done.3
  37.0 0.2 convolution_bitcast_fusion.1.refs_6_
  37.2 0.5 copy-done.6
  37.7 0.1 convert_reduce_fusion
  37.8 0.2 convert_reduce_fusion.1
  38.0 0.3 convolution_bitcast_fusion
  38.4 0.0 copy-start.9
  38.4 0.1 copy.73.refs_9_
  38.5 0.6 copy-done.9
  39.1 0.7 copy-done.13
  39.7 0.1 select_reduce_fusion.4
  39.8 0.1 select_reduce_fusion.1
  39.9 0.1 select_reduce_fusion.2
  40.0 1.1 %shard_map.146 = (f32[56,1152]{1,0:T(8,128)S(1)}, f32[4,216,128]{2,1,0:T(8,128)S(1)}) custom-call(f32[9,56,128]{2,1,0:T(8,128)S(1)} %bitcast.60, f32[56,1152]{1,0:T(8,128)S(1)} %get-tuple-element.27.refs_1_, f32[4,216,128]{2,1,0:T(8,128)S(1)} %get-tuple-element.28.refs_2_, f32[408,128]{1,0:T(8,128)S(1)} %get-tuple-element.29.refs_3_.refs_6_, ...), custom_call_target="tpu_custom_call" | custom-call | tf_op jit(solution)/shard_map/pallas_call | solution.py:273
  41.1 0.1 add_bitcast_fusion.refs_11_
  41.2 1.9 %shard_map.147 = (f32[56,1152]{1,0:T(8,128)S(1)}, f32[256,128]{1,0:T(8,128)}) custom-call(f32[56,1152]{1,0:T(8,128)S(1)} %get-tuple-element.30.refs_0_, f32[4,216,128]{2,1,0:T(8,128)S(1)} %get-tuple-element.31.refs_1_, f32[112,128]{1,0:T(8,128)S(1)} %collective-permute-done.refs_2_, f32[112,128]{1,0:T(8,128)S(1)} %collective-permute-done.1.refs_3_, ...), custom_call_target="tpu_custom_call" | custom-call | tf_op jit(solution)/shard_map/pallas_call | solution.py:273
  43.1 9.5 %all-to-all-start = ((f32[32,8,128]{2,1,0:T(8,128)}), f32[32,8,128]{2,1,0:T(8,128)S(1)}, u32[]{:S(2)}, u32[]{:S(2)}) async-start(f32[32,8,128]{2,1,0:T(8,128)} %bitcast.24), calls=%async_computation | async-start | bytes 262144 | tf_op jit(solution)/shard_map/all_to_all | solution.py:397
  52.6 0.1 select_reduce_fusion
  52.7 15.7 %all-to-all-done = f32[32,8,128]{2,1,0:T(8,128)S(1)} async-done(((f32[32,8,128]{2,1,0:T(8,128)}), f32[32,8,128]{2,1,0:T(8,128)S(1)}, u32[]{:S(2)}, u32[]{:S(2)}) %all-to-all-start) | async-done | bytes 131104 | tf_op jit(solution)/shard_map/all_to_all | solution.py:397
  68.5 6.6 %shard_map.148 = (f32[56,1152]{1,0:T(8,128)S(1)}, f32[4,216,128]{2,1,0:T(8,128)S(1)}, f32[112,128]{1,0:T(8,128)S(1)}, f32[112,128]{1,0:T(8,128)S(1)}, f32[112,12...) custom-call(f32[56,1152]{1,0:T(8,128)S(1)} %get-tuple-element.37.refs_0_, ...), custom_call_target="tpu_custom_call" | custom-call | tf_op jit(solution)/shard_map/pallas_call | solution.py:273
  75.0 1.9 %collective-permute-start.4 = (f32[112,128]{1,0:T(8,128)S(1)}, f32[112,128]{1,0:T(8,128)S(1)}, u32[]{:S(2)}, u32[]{:S(2)}) collective-permute-start(f32[112,128]{1,0:T(8,128)S(1)} %get-tuple-element.45), channel_id=1, source_target_pairs={{0,32},{32,64},{64,96},{96,128},{128,160},{160,192},{192,224},{224... | collective-permute-start | bytes 172040 | tf_op jit(solution)/shard_map/ppermute | solution.py:289
  77.0 6.7 %collective-permute-start.5 = (f32[112,128]{1,0:T(8,128)S(1)}, f32[112,128]{1,0:T(8,128)S(1)}, u32[]{:S(2)}, u32[]{:S(2)}) collective-permute-start(f32[112,128]{1,0:T(8,128)S(1)} %get-tuple-element.46), channel_id=1, source_target_pairs={{32,0},{64,32},{96,64},{128,96},{160,128},{192,160},{224,192},{256... | collective-permute-start | bytes 172040 | tf_op jit(solution)/shard_map/ppermute | solution.py:289
  83.7 2.1 %collective-permute-start.6 = (f32[112,128]{1,0:T(8,128)S(1)}, f32[112,128]{1,0:T(8,128)S(1)}, u32[]{:S(2)}, u32[]{:S(2)}) collective-permute-start(f32[112,128]{1,0:T(8,128)S(1)} %get-tuple-element.47), channel_id=1, source_target_pairs={{0,1},{1,2},{2,3},{3,4},{4,5},{5,6},{6,7},{7,8},{8,9},{9,10},{10,1... | collective-permute-start | bytes 172040 | tf_op jit(solution)/shard_map/ppermute | solution.py:289
  85.7 0.1 collective-permute-start.7
  85.9 1.1 %shard_map.149 = (f32[56,1152]{1,0:T(8,128)S(1)}, f32[4,216,128]{2,1,0:T(8,128)S(1)}) custom-call(f32[56,1152]{1,0:T(8,128)S(1)} %get-tuple-element.39.refs_0_, f32[56,1152]{1,0:T(8,128)S(1)} %get-tuple-element.40.refs_1_, f32[4,216,128]{2,1,0:T(8,128)S(1)} %get-tuple-element.41.refs_2_, f32[408,128]{1,0:T(8,128)S(1)} %get-tuple-element.42.refs_3_.refs_6_, ...), custom_call_target="tpu_custom_call" | custom-call | tf_op jit(solution)/shard_map/pallas_call | solution.py:273
  87.0 2.6 %collective-permute-done.7.refs_5_ = f32[112,128]{1,0:T(8,128)S(1)} collective-permute-done((f32[112,128]{1,0:T(8,128)S(1)}, f32[112,128]{1,0:T(8,128)S(1)}, u32[]{:S(2)}, u32[]{:S(2)}) %collective-permute-start.7) | collective-permute-done | bytes 57376 | tf_op jit(solution)/shard_map/ppermute | solution.py:289
  89.6 1.7 %shard_map.150 = f32[9,56,128]{2,1,0:T(8,128)} custom-call(f32[56,1152]{1,0:T(8,128)S(1)} %get-tuple-element.43.refs_0_, f32[4,216,128]{2,1,0:T(8,128)S(1)} %get-tuple-element.44.refs_1_, f32[112,128]{1,0:T(8,128)S(1)} %collective-permute-done.4.refs_2_, f32[112,128]{1,0:T(8,128)S(1)} %collective-permute-done.5.refs_3_, ...), custom_call_target="tpu_custom_call" | custom-call | tf_op jit(solution)/shard_map/pallas_call | solution.py:273
  (44 shorter events, 0.2 us)
Async XLA Ops:
  0.0 38.0 %copy-start = (f32[3,21,21]{2,1,0:T(8,128)S(1)}, f32[3,21,21]{2,1,0:T(8,128)}, u32[]{:S(2)}) copy-start(f32[3,21,21]{2,1,0:T(8,128)} %param.24) | copy-start | bytes 15880
  1.1 0.9 copy-start.5
  2.2 0.9 copy-start.2
  3.2 0.8 copy-start.4
  4.0 0.7 copy-start.7
  4.0 1.5 %copy-start.12 = (s32[1,128]{1,0:T(1,128)S(1)}, s32[1,128]{1,0:T(1,128)}, u32[]{:S(2)}) copy-start(s32[1,128]{1,0:T(1,128)} %param.17) | copy-start | bytes 1540
  4.0 1.6 %copy-start.11 = (f32[8]{0:T(128)S(1)}, f32[8]{0:T(128)}, u32[]{:S(2)}) copy-start(f32[8]{0:T(128)} %param.20) | copy-start | bytes 100
  4.7 0.7 copy-start.10
  5.4 0.9 %copy-start.1 = (f32[1,56,9,128]{3,1,2,0:T(8,128)S(1)}, f32[1,56,9,128]{3,1,2,0:T(8,128)}, u32[]{:S(2)}) copy-start(f32[1,56,9,128]{3,1,2,0:T(8,128)} %param.15) | copy-start | bytes 774148
  12.8 28.5 %collective-permute-start = (f32[112,128]{1,0:T(8,128)S(1)}, f32[112,128]{1,0:T(8,128)S(1)}, u32[]{:S(2)}, u32[]{:S(2)}) collective-permute-start(f32[112,128]{1,0:T(8,128)S(1)} %get-tuple-element.32), channel_id=1, source_target_pairs={{0,32},{32,64},{64,96},{96,128},{128,160},{160,192},{192,224},{224... | collective-permute-start | bytes 172040 | tf_op jit(solution)/shard_map/ppermute | solution.py:289
  16.8 24.4 %collective-permute-start.1 = (f32[112,128]{1,0:T(8,128)S(1)}, f32[112,128]{1,0:T(8,128)S(1)}, u32[]{:S(2)}, u32[]{:S(2)}) collective-permute-start(f32[112,128]{1,0:T(8,128)S(1)} %get-tuple-element.33), channel_id=1, source_target_pairs={{32,0},{64,32},{96,64},{128,96},{160,128},{192,160},{224,192},{256... | collective-permute-start | bytes 172040 | tf_op jit(solution)/shard_map/ppermute | solution.py:289
  22.8 13.3 %copy-start.8 = (s32[2,1,512]{2,1,0:T(1,128)S(1)}, s32[2,1,512]{2,1,0:T(1,128)}, u32[]{:S(2)}) copy-start(s32[2,1,512]{2,1,0:T(1,128)} %param.25) | copy-start | bytes 12292
  22.8 18.4 %collective-permute-start.2 = (f32[112,128]{1,0:T(8,128)S(1)}, f32[112,128]{1,0:T(8,128)S(1)}, u32[]{:S(2)}, u32[]{:S(2)}) collective-permute-start(f32[112,128]{1,0:T(8,128)S(1)} %get-tuple-element.34), channel_id=1, source_target_pairs={{0,1},{1,2},{2,3},{3,4},{4,5},{5,6},{6,7},{7,8},{8,9},{9,10},{10,1... | collective-permute-start | bytes 172040 | tf_op jit(solution)/shard_map/ppermute | solution.py:289
  25.8 15.4 %collective-permute-start.3 = (f32[112,128]{1,0:T(8,128)S(1)}, f32[112,128]{1,0:T(8,128)S(1)}, u32[]{:S(2)}, u32[]{:S(2)}) collective-permute-start(f32[112,128]{1,0:T(8,128)S(1)} %get-tuple-element.35), channel_id=1, source_target_pairs={{1,0},{2,1},{3,2},{4,3},{5,4},{6,5},{7,6},{8,7},{9,8},{10,9},{11,1... | collective-permute-start | bytes 172040 | tf_op jit(solution)/shard_map/ppermute | solution.py:289
  36.2 0.8 copy-start.3
  37.0 0.7 copy-start.6
  38.4 0.7 copy-start.9
  39.1 0.7 copy-start.13
  43.1 25.4 %all-to-all-start = ((f32[32,8,128]{2,1,0:T(8,128)}), f32[32,8,128]{2,1,0:T(8,128)S(1)}, u32[]{:S(2)}, u32[]{:S(2)}) async-start(f32[32,8,128]{2,1,0:T(8,128)} %bitcast.24), calls=%async_computation | async-start | bytes 262144 | tf_op jit(solution)/shard_map/all_to_all | solution.py:397
  75.0 12.0 %collective-permute-start.4 = (f32[112,128]{1,0:T(8,128)S(1)}, f32[112,128]{1,0:T(8,128)S(1)}, u32[]{:S(2)}, u32[]{:S(2)}) collective-permute-start(f32[112,128]{1,0:T(8,128)S(1)} %get-tuple-element.45), channel_id=1, source_target_pairs={{0,32},{32,64},{64,96},{96,128},{128,160},{160,192},{192,224},{224... | collective-permute-start | bytes 172040 | tf_op jit(solution)/shard_map/ppermute | solution.py:289
  77.0 10.0 %collective-permute-start.5 = (f32[112,128]{1,0:T(8,128)S(1)}, f32[112,128]{1,0:T(8,128)S(1)}, u32[]{:S(2)}, u32[]{:S(2)}) collective-permute-start(f32[112,128]{1,0:T(8,128)S(1)} %get-tuple-element.46), channel_id=1, source_target_pairs={{32,0},{64,32},{96,64},{128,96},{160,128},{192,160},{224,192},{256... | collective-permute-start | bytes 172040 | tf_op jit(solution)/shard_map/ppermute | solution.py:289
  83.7 3.4 %collective-permute-start.6 = (f32[112,128]{1,0:T(8,128)S(1)}, f32[112,128]{1,0:T(8,128)S(1)}, u32[]{:S(2)}, u32[]{:S(2)}) collective-permute-start(f32[112,128]{1,0:T(8,128)S(1)} %get-tuple-element.47), channel_id=1, source_target_pairs={{0,1},{1,2},{2,3},{3,4},{4,5},{5,6},{6,7},{7,8},{8,9},{9,10},{10,1... | collective-permute-start | bytes 172040 | tf_op jit(solution)/shard_map/ppermute | solution.py:289
  85.7 3.9 %collective-permute-start.7 = (f32[112,128]{1,0:T(8,128)S(1)}, f32[112,128]{1,0:T(8,128)S(1)}, u32[]{:S(2)}, u32[]{:S(2)}) collective-permute-start(f32[112,128]{1,0:T(8,128)S(1)} %get-tuple-element.48), channel_id=1, source_target_pairs={{1,0},{2,1},{3,2},{4,3},{5,4},{6,5},{7,6},{8,7},{9,8},{10,9},{11,1... | collective-permute-start | bytes 172040 | tf_op jit(solution)/shard_map/ppermute | solution.py:289
where the time goes:
time: 92 us; the launch traced here: 91.4 us
  starting transfers between devices  43.7 us (48%)
  Pallas kernels  18.8 us (20%)
  waiting for transfers between devices  18.4 us (20%)
  local copies, waits for them, and re-layouts  8.58 us (9%)
  other arithmetic  1.05 us (1%)
    ppermute x8, starting transfers between devices, exchange(): out += [lax.ppermute(higher, axis, up), lax.ppermute(lower, axis, down)]  34.2 us
    pallas_call x6, Pallas kernels, call(): pl.pallas_call(lambda *refs: body(refs), out_shape=[jax.ShapeDtypeStruct(...  18.8 us
    all_to_all x1, waiting for transfers between devices, shards(): lax.all_to_all(packed, 'dom', split_axis=0, concat_axis=0, tiled=True)  15.7 us
    all_to_all x1, starting transfers between devices, shards(): lax.all_to_all(packed, 'dom', split_axis=0, concat_axis=0, tiled=True)  9.49 us
    unnamed x31, local copies, waits for them, and re-layouts  6.7 us
    ppermute x8, waiting for transfers between devices, exchange(): out += [lax.ppermute(higher, axis, up), lax.ppermute(lower, axis, down)]  2.64 us
  transfers between devices with their start and end apart: 9, of which 2 were waited for; matrix products, arithmetic and copies ran while one was open for 2% of the time, Pallas kernels for 2%

commit v1 on v0

v1 whole, which is shorter than its diff:
```python
import functools

import jax
import jax.numpy as jnp
from jax import lax
from jax.experimental import pallas as pl
from jax.experimental.pallas import tpu as pltpu
from jax.sharding import PartitionSpec as P

TAYLOR = 6
FIELDS = 9
LANES = 128
FACE_PAD = 24
TRACE_ROWS = FIELDS * FACE_PAD
MSG_ROWS = 112
COEF_PAD = 16
STAR_ROWS = 27 * COEF_PAD
FLUX_ROWS = 18 * COEF_PAD
VALUES = 512

highest = lax.Precision.HIGHEST
friction_coef = 0.6
relax_share = 0.5
f32 = jnp.float32
bf16 = jnp.bfloat16


def halves(x):
    hi = x.astype(bf16)
    return hi, (x - hi.astype(f32)).astype(bf16)


def left_matrix(a):
    hi, lo = halves(a)
    both = jnp.concatenate([hi.astype(f32), lo.astype(f32)], axis=0).astype(bf16)
    return both, hi


def mm(left, x):
    both, hi = left
    x_hi, x_lo = halves(x)
    rows = hi.shape[0]
    first = jnp.dot(both, x_hi, preferred_element_type=f32)
    return first[:rows] + (first[rows:] + jnp.dot(hi, x_lo, preferred_element_type=f32))


def lane_gather(x, lane):
    return jnp.take_along_axis(x, jnp.broadcast_to(lane, x.shape), axis=1, mode="promise_in_bounds")


def block(f):
    return slice(f * LANES, (f + 1) * LANES)


def exact_dot(a, hot):
    total = None
    for _ in range(3):
        part = a.astype(bf16)
        a = a - part.astype(f32)
        term = jnp.dot(part, hot, preferred_element_type=f32)
        total = term if total is None else total + term
    return total


def coefficient_rows(table, hot):
    count = table.shape[0] // 8
    size = -(-table.shape[0] // LANES) * LANES
    wide = jnp.concatenate([table, jnp.zeros((table.shape[0], LANES - FIELDS), f32)], axis=1)
    if size > table.shape[0]:
        wide = jnp.concatenate([wide, jnp.zeros((size - table.shape[0], LANES), f32)], axis=0)
    turned = jnp.transpose(wide, (1, 0))[:COEF_PAD]
    stacked = jnp.concatenate([turned] * count, axis=0)
    pair = lax.broadcasted_iota(jnp.int32, stacked.shape, 0) // COEF_PAD
    at = lax.broadcasted_iota(jnp.int32, stacked.shape, 1) // 8
    many = jnp.concatenate([hot] * (size // 8), axis=0).astype(bf16)
    return exact_dot(jnp.where(pair == at, stacked, 0.0), many)


def spread_rows(ops_ref, first, count, wide_ref, start=0):
    for p in range(count):
        for g in range(FIELDS):
            r = (first + p) * COEF_PAD + g
            wide_ref[start + p * FIELDS + g] = jnp.broadcast_to(ops_ref[r : r + 1, :], (8, LANES))


def mix(load, wide_ref, start, outs):
    accs = [None] * len(outs)
    for f in range(FIELDS):
        value = load(f)
        rows = value.shape[0]
        value = value.reshape(rows // 8, 8, LANES)
        for t, g in enumerate(outs):
            part = value * wide_ref[start + f * FIELDS + g][None]
            accs[t] = part if accs[t] is None else accs[t] + part
    return [a.reshape(-1, LANES) for a in accs]


GROUPS_OF_FIELDS = ((0, 1), (2, 3), (4, 5), (6, 7), (8,))


def star_mixed(src_ref, wide_ref, outs):
    load = lambda f: src_ref[:, block(f)]
    parts = []
    for d in range(3):
        parts.append(jnp.concatenate(mix(load, wide_ref, d * 81, outs), axis=1))
    return jnp.concatenate(parts, axis=0)


def fetch(pairs, sems):
    copies = [pltpu.make_async_copy(a, b, sems.at[n]) for n, (a, b) in enumerate(pairs)]
    for copy in copies:
        copy.start()
    for copy in copies:
        copy.wait()


def one_hot(desc):
    kinds = lax.broadcasted_iota(jnp.int32, (8, LANES), 0).astype(f32)
    return (jnp.broadcast_to(desc[3:4], (8, LANES)) == kinds).astype(f32)


def first_half_body(place, refs):
    phase = 1 if place else 0
    if place:
        (state_ref, recv_ref, maps_ref, desc_ref, star_ref, send_ref, stiff_ref, project_ref,
         integral_ref, trace_ref, m0, m1, m2, m3, ops_ref, hot_ref, placed_ref,
         wide_ref, deriv_ref, padded_ref) = refs
    else:
        (state_in, geometry_in, material_in, star_in, send_in, stiff_in, project_in,
         integral_ref, trace_ref, m0, m1, m2, m3, ops_ref, hot_ref, desc_ref,
         wide_ref, deriv_ref, padded_ref,
         state_ref, geometry_ref, material_ref, star_ref, send_ref, stiff_ref, project_ref,
         sems) = refs
        fetch(
            [(state_in, state_ref), (geometry_in, geometry_ref), (material_in, material_ref),
             (star_in, star_ref), (send_in, send_ref), (stiff_in, stiff_ref),
             (project_in, project_ref)],
            sems,
        )
        desc_ref[...] = jnp.zeros((8, LANES), f32)
        for d in range(3):
            desc_ref[d : d + 1, :] = geometry_ref[d]
        desc_ref[3:4, :] = material_ref[...].astype(f32)
    modes = stiff_ref.shape[1]

    desc = desc_ref[...]
    if place:
        arriving = maps_ref[1:2, :]
        arrives = arriving >= 0
        lane = jnp.maximum(arriving, 0)
        moved = []
        for b in range(4):
            got = recv_ref[pl.ds(b, 64, stride=4), :]
            got = jnp.concatenate([got, got], axis=0)
            moved.append(lane_gather(jnp.transpose(got, (1, 0)), lane))
        moved = jnp.concatenate(moved, axis=0)
        for f in range(FIELDS):
            new = jnp.where(arrives, moved[f * modes : (f + 1) * modes], state_ref[:, block(f)])
            placed_ref[:, block(f)] = new
        desc = jnp.where(arrives, moved[FIELDS * modes :], desc)
        integral_ref[...] = placed_ref[...]
    else:
        for f in range(FIELDS):
            integral_ref[:, block(f)] = state_ref[f]

    hot = one_hot(desc)
    hot_ref[...] = hot
    rows = coefficient_rows(star_ref[...], hot)
    row_at = lax.broadcasted_iota(jnp.int32, (STAR_ROWS, LANES), 0)
    third = STAR_ROWS // 3
    scale = jnp.where(row_at < third, desc[0:1], jnp.where(row_at < 2 * third, desc[1:2], desc[2:3]))
    ops_ref[...] = rows * scale
    spread_rows(ops_ref, 0, 27, wide_ref)

    across = jnp.concatenate([jnp.transpose(stiff_ref[d], (1, 0)) for d in range(3)], axis=0)
    stiff = left_matrix(-jnp.transpose(across, (1, 0)))
    deriv_ref[0] = integral_ref[...]

    def degree(j, coef):
        now = deriv_ref.at[j % 2]
        later = deriv_ref.at[(j + 1) % 2]
        for outs in GROUPS_OF_FIELDS:
            new = mm(stiff, star_mixed(now, wide_ref, outs))
            lanes = slice(outs[0] * LANES, (outs[-1] + 1) * LANES)
            later[:, lanes] = new
            integral_ref[:, lanes] = integral_ref[:, lanes] + new * coef

    coef = 1.0
    for j in range(TAYLOR - 1):
        coef = coef / (j + 2)
        degree(j, coef)

    padded_ref[...] = jnp.zeros(padded_ref.shape, f32)
    for i in range(4):
        padded_ref[i * FACE_PAD : i * FACE_PAD + project_ref.shape[0], :] = project_ref[:, i, :]
    project = left_matrix(padded_ref[...])
    for outs in GROUPS_OF_FIELDS:
        lanes = slice(outs[0] * LANES, (outs[-1] + 1) * LANES)
        traced = mm(project, integral_ref[:, lanes])
        for t, f in enumerate(outs):
            for i in range(4):
                trace_ref[i, f * FACE_PAD : (f + 1) * FACE_PAD, :] = traced[
                    i * FACE_PAD : (i + 1) * FACE_PAD, block(t)
                ]

    low = lax.broadcasted_iota(jnp.int32, (8, LANES), 1) < 64
    for c, msg_ref in enumerate((m0, m1, m2, m3)):
        row = send_ref[phase, 0, c : c + 1, :]
        index = jnp.broadcast_to(jnp.concatenate([row, row], axis=1), (8, LANES))
        lane, face = index & 127, index >> 7
        for r in range(MSG_ROWS // 8):
            out = None
            for i in range(4):
                got = lane_gather(trace_ref[i, r * 8 : r * 8 + 8, :], lane)
                high_row = r * 8 + MSG_ROWS
                if high_row < TRACE_ROWS:
                    other = lane_gather(trace_ref[i, high_row : high_row + 8, :], lane)
                    got = jnp.where(low, got, other)
                out = got if out is None else jnp.where(face == i, got, out)
            msg_ref[r * 8 : r * 8 + 8, :] = out


def to_column(row, size):
    square = (size, row.shape[1])
    diagonal = lax.broadcasted_iota(jnp.int32, square, 0) == lax.broadcasted_iota(
        jnp.int32, square, 1
    )
    return jnp.sum(jnp.where(diagonal, row, 0.0), axis=1, keepdims=True)


def migration_maps(slots, owners, my_dom):
    doms, leave = owners.shape
    capacity = 2 * leave // doms
    total = capacity * doms
    iota = lambda shape, dim: lax.broadcasted_iota(jnp.int32, shape, dim)
    owner = jnp.sum(
        jnp.where(iota(owners.shape, 0) == my_dom, owners, 0).astype(f32), axis=0, keepdims=True
    )
    owner_col = to_column(owner, leave)
    slots_col = to_column(slots.astype(f32), leave)
    square = (leave, leave)
    before = (owner == owner_col) & (iota(square, 1) < iota(square, 0))
    rank = jnp.sum(jnp.where(before, 1.0, 0.0), axis=1, keepdims=True)
    send_slot = owner_col * capacity + rank
    wide = (leave, LANES)
    slot = (iota(wide, 1) % total).astype(f32)
    source = jnp.sum(jnp.where(send_slot == slot, slots_col, 0.0), axis=0, keepdims=True)

    arrivals = jnp.sum(jnp.where(owners == my_dom, 1.0, 0.0), axis=1, keepdims=True)
    wide = (doms, LANES)
    sender = iota(wide, 1) // capacity
    mine = jnp.sum(jnp.where(iota(wide, 0) == sender, arrivals, 0.0), axis=0, keepdims=True)
    ahead = jnp.sum(jnp.where(iota(wide, 0) < sender, arrivals, 0.0), axis=0, keepdims=True)
    lane = iota((1, LANES), 1)
    within = (lane % capacity).astype(f32)
    position = jnp.where((lane < total) & (within < mine), ahead + within, -1.0)
    position_col = to_column(position, LANES)
    wide = (leave, LANES)
    here = slots_col == iota(wide, 1).astype(f32)
    order = iota(wide, 0).astype(f32) + 1.0
    number = jnp.sum(jnp.where(here, order, 0.0), axis=0, keepdims=True) - 1.0
    wide = (LANES, LANES)
    hit = (position_col == number) & (jnp.broadcast_to(number, wide) >= 0.0)
    arriving = jnp.sum(
        jnp.where(hit, iota(wide, 0).astype(f32) + 1.0, 0.0), axis=0, keepdims=True
    )
    return source.astype(jnp.int32), arriving.astype(jnp.int32) - 1


def middle_body(phase, refs):
    (state_ref, integral_ref, trace_ref, ops_ref, hot_ref, near_ref, _, stiff_ref, flux_ref,
     cohesion_ref) = refs[:10]
    if phase == 0:
        (lift_in, project_ref, reorient_ref, slots_ref, owners_ref,
         partial_ref, local_ref, flux_rows_ref, own_ref, lift_ref, maps_ref,
         wide_ref, columns_ref) = refs[10:]
        own_ref[...] = sum(
            jnp.dot(
                jnp.transpose(lift_in[:, i, :], (1, 0)), project_ref[:, i, :],
                precision=highest, preferred_element_type=f32,
            )
            for i in range(4)
        )
        columns_ref[...] = jnp.zeros(columns_ref.shape, f32)
        face_modes = reorient_ref.shape[1]
        for h in range(3):
            back = jnp.transpose(reorient_ref[h], (1, 0))
            for i in range(4):
                at = (i * 3 + h) * FACE_PAD
                columns_ref[at : at + face_modes, :] = jnp.dot(
                    back, lift_in[:, i, :], precision=highest, preferred_element_type=f32
                )
        lift_ref[...] = jnp.transpose(columns_ref[...], (1, 0))
        source, arriving = migration_maps(slots_ref[...], owners_ref[...], lax.axis_index("dom"))
        maps_ref[0:1, :] = source
        maps_ref[1:2, :] = arriving
    else:
        own_ref, partial_ref, local_ref, flux_rows_ref, wide_ref = refs[10:]
    modes = stiff_ref.shape[1]
    hot = hot_ref[...]
    flux_rows_ref[0:FLUX_ROWS, :] = coefficient_rows(flux_ref[...], hot)
    yield_rows = exact_dot(jnp.broadcast_to(cohesion_ref[...], (8, 8)), hot.astype(bf16))
    flux_rows_ref[FLUX_ROWS : FLUX_ROWS + 8, :] = yield_rows
    spread_rows(ops_ref, 0, 27, wide_ref)
    spread_rows(flux_rows_ref, 0, 9, wide_ref, 243)
    volume = left_matrix(jnp.transpose(stiff_ref[...].reshape(3 * modes, modes), (1, 0)))
    own = left_matrix(own_ref[...])
    for outs in GROUPS_OF_FIELDS:
        lanes = slice(outs[0] * LANES, (outs[-1] + 1) * LANES)
        load = lambda f: integral_ref[:, block(f)]
        added = mm(volume, star_mixed(integral_ref, wide_ref, outs))
        flux = mm(own, jnp.concatenate(mix(load, wide_ref, 243, outs), axis=1))
        if len(state_ref.shape) == 3:
            before = jnp.concatenate([state_ref[g] for g in outs], axis=1)
        else:
            before = state_ref[:, lanes]
        partial_ref[:, lanes] = before + added - flux
    for i in range(4):
        index = jnp.broadcast_to(near_ref[phase, :, block(i)], (8, LANES))
        lane, source = index & 127, index >> 7
        for r in range(TRACE_ROWS // 8):
            rows = slice(r * 8, r * 8 + 8)
            out = None
            for j in range(4):
                got = lane_gather(trace_ref[j, rows, :], lane)
                out = got if out is None else jnp.where(source == j, got, out)
            local_ref[i, rows, :] = out


def last_half_body(pack, refs):
    phase = 0 if pack else 1
    if pack:
        (partial_ref, local_ref, m0, m1, m2, m3, ops_ref, near_ref, orient_ref, lift_ref,
         desc_ref, maps_ref, out_ref, packed_ref, wide_ref, both_ref, turned_ref, sum_ref) = refs
    else:
        (partial_ref, local_ref, m0, m1, m2, m3, ops_ref, near_ref, orient_ref, lift_ref,
         out_ref, wide_ref, both_ref, turned_ref, sum_ref) = refs
    modes = lift_ref.shape[0]
    spread_rows(ops_ref, 9, 9, wide_ref)

    low = lax.broadcasted_iota(jnp.int32, (MSG_ROWS, LANES), 1) < 64
    rest = TRACE_ROWS - MSG_ROWS
    for k, (a, b) in enumerate(((m0, m1), (m2, m3))):
        first, second = a[...], b[...]
        both_ref[k, 0:MSG_ROWS, :] = jnp.where(low, first, pltpu.roll(second, 64, 1))
        upper = jnp.where(low, pltpu.roll(first, 64, 1), second)
        both_ref[k, MSG_ROWS:TRACE_ROWS, :] = upper[:rest]

    for i in range(4):
        index = jnp.broadcast_to(near_ref[phase, :, block(i)], (8, LANES))
        lane, source = index & 127, index >> 7
        for r in range(TRACE_ROWS // 8):
            rows = slice(r * 8, r * 8 + 8)
            out = local_ref[i, rows, :]
            for k in range(2):
                out = jnp.where(source == 4 + k, lane_gather(both_ref[k, rows, :], lane), out)
            turned_ref[i, rows, :] = out

    lift = left_matrix(lift_ref[...])
    for outs in GROUPS_OF_FIELDS:
        lanes = slice(outs[0] * LANES, (outs[-1] + 1) * LANES)
        pieces = []
        for i in range(4):
            load = lambda f: turned_ref[i, f * FACE_PAD : (f + 1) * FACE_PAD, :]
            mixed = mix(load, wide_ref, 0, outs)
            orient = jnp.broadcast_to(orient_ref[phase, :, block(i)], (FACE_PAD, LANES))
            for h in range(3):
                pieces.append(
                    jnp.concatenate([jnp.where(orient == h, m, 0.0) for m in mixed], axis=1)
                )
        flux = mm(lift, jnp.concatenate(pieces, axis=0))
        wide_out = partial_ref[:, lanes] - flux
        for t, g in enumerate(outs):
            sum_ref[:, block(g)] = wide_out[:, block(t)]

    zero = [sum_ref[0:1, block(f)] for f in range(6)]
    pressure_zero = -(zero[0] + zero[1] + zero[2]) / 3.0
    second = 0.5 * sum((zero[f] + pressure_zero) * (zero[f] + pressure_zero) for f in range(3))
    second = second + sum(zero[f] * zero[f] for f in range(3, 6))
    shear_mag = jnp.sqrt(second)
    yield_row = ops_ref[FLUX_ROWS : FLUX_ROWS + 1, :]
    yield_stress = yield_row + friction_coef * jnp.maximum(pressure_zero, 0.0)
    factor = 1.0 - relax_share * jnp.maximum(
        0.0, 1.0 - yield_stress / jnp.maximum(shear_mag, yield_stress)
    )
    normals = [sum_ref[:, block(f)] for f in range(3)]
    pressure = -(normals[0] + normals[1] + normals[2]) / 3.0
    fields = [-pressure + factor * (n + pressure) for n in normals]
    fields += [factor * sum_ref[:, block(f)] for f in range(3, 6)]
    fields += [sum_ref[:, block(f)] for f in range(6, FIELDS)]
    if not pack:
        for f in range(FIELDS):
            out_ref[f] = fields[f]
        return
    for f in range(FIELDS):
        out_ref[:, block(f)] = fields[f]
    values = jnp.concatenate(fields + [desc_ref[...]], axis=0)
    leaving = lane_gather(values, maps_ref[0:1, :])
    for b in range(4):
        turned = jnp.transpose(leaving[b * LANES : (b + 1) * LANES], (1, 0))
        packed_ref[pl.ds(b, 64, stride=4), :] = turned[:64]


def call(body, outs, scratch, *args, raw=False):
    space = pltpu.HBM if raw else pltpu.VMEM
    scratch = [pltpu.VMEM(s, f32) for s in scratch]
    if raw:
        scratch += [pltpu.VMEM(a.shape, a.dtype) for a in args]
        scratch += [pltpu.SemaphoreType.DMA((len(args),))]
    outs = [s if isinstance(s, jax.ShapeDtypeStruct) else jax.ShapeDtypeStruct(s, f32) for s in outs]
    return pl.pallas_call(
        lambda *refs: body(refs),
        out_shape=outs,
        in_specs=[pl.BlockSpec(memory_space=space)] * len(args),
        out_specs=[pl.BlockSpec(memory_space=pltpu.VMEM)] * len(outs),
        scratch_shapes=scratch,
        compiler_params=pltpu.CompilerParams(vmem_limit_bytes=48 << 20),
    )(*[pltpu.with_memory_space_constraint(a, pltpu.HBM) for a in args] if raw else args)


def exchange(messages):
    out = []
    for axis, (lower, higher) in (("group", messages[:2]), ("dom", messages[2:])):
        size = lax.axis_size(axis)
        up = [(i, (i + 1) % size) for i in range(size)]
        down = [(j, i) for i, j in up]
        out += [lax.ppermute(higher, axis, up), lax.ppermute(lower, axis, down)]
    return out


def shards(
    modal_state,
    geometry,
    material,
    star_table,
    flux_table,
    cohesion,
    stiffness,
    face_project,
    face_lift,
    reorient,
    neighbour_face,
    send_faces,
    orientation,
    leaving_slots,
    leaving_owner,
):
    modes, nfield, elem_count = modal_state.shape[1:]
    kinds = star_table.shape[0]
    state = jnp.transpose(modal_state[0], (1, 0, 2))
    star = jnp.transpose(star_table, (1, 2, 0, 3)).reshape(3 * nfield * kinds, nfield)
    flux = jnp.transpose(flux_table, (1, 2, 0, 3)).reshape(2 * nfield * kinds, nfield)
    cohesion = cohesion[None, :]
    geometry = jnp.transpose(geometry, (1, 0, 2))
    face_project = jnp.transpose(face_project, (1, 0, 2))
    face_lift = jnp.transpose(face_lift, (2, 0, 1))

    full = (modes, nfield * elem_count)
    traces = (4, TRACE_ROWS, LANES)
    msg = (MSG_ROWS, LANES)
    tile = (8, LANES)
    ops_shape = (STAR_ROWS, LANES)
    flux_shape = (FLUX_ROWS + 8, LANES)
    wide = (243, 8, LANES)
    wide_more = (324, 8, LANES)
    wide_flux = (81, 8, LANES)
    lift_shape = (modes, 12 * FACE_PAD)
    maps_shape = jax.ShapeDtypeStruct((2, LANES), jnp.int32)
    first_scratch = [wide, (2,) + full, (4 * FACE_PAD, modes)]

    integral, trace, a, b, c, d, ops, hot, desc = call(
        functools.partial(first_half_body, False),
        [full, traces, msg, msg, msg, msg, ops_shape, tile, tile],
        first_scratch,
        state, geometry, material, star, send_faces, stiffness, face_project,
        raw=True,
    )
    incoming = exchange([a, b, c, d])
    partial, local, flux_rows, own, lift, maps = call(
        functools.partial(middle_body, 0),
        [full, traces, flux_shape, (modes, modes), lift_shape, maps_shape],
        [wide_more, (12 * FACE_PAD, modes)],
        state, integral, trace, ops, hot, neighbour_face, orientation, stiffness, flux, cohesion,
        face_lift, face_project, reorient, leaving_slots, leaving_owner,
    )
    stepped, packed = call(
        functools.partial(last_half_body, True),
        [full, (256, LANES)],
        [wide_flux, (2,) + traces[1:], traces, full],
        partial, local, *incoming, flux_rows, neighbour_face, orientation, lift, desc, maps,
    )
    moved = lax.all_to_all(packed, "dom", split_axis=0, concat_axis=0, tiled=True)
    integral, trace, a, b, c, d, ops, hot, placed = call(
        functools.partial(first_half_body, True),
        [full, traces, msg, msg, msg, msg, ops_shape, tile, full],
        first_scratch,
        stepped, moved, maps, desc, star, send_faces, stiffness, face_project,
    )
    incoming = exchange([a, b, c, d])
    partial, local, flux_rows = call(
        functools.partial(middle_body, 1),
        [full, traces, flux_shape],
        [wide_more],
        placed, integral, trace, ops, hot, neighbour_face, orientation, stiffness, flux,
        cohesion, own,
    )
    (final,) = call(
        functools.partial(last_half_body, False),
        [(nfield, modes, elem_count)],
        [wide_flux, (2,) + traces[1:], traces, full],
        partial, local, *incoming, flux_rows, neighbour_face, orientation, lift,
    )
    return jnp.transpose(final, (1, 0, 2))[None]


def solution(mesh):
    in_specs = (
        P(("group", "dom"), None, None, None),
        P(("group", "dom"), None, None),
        P(("group", "dom"), None),
        P(),
        P(),
        P(),
        P(),
        P(),
        P(),
        P(),
        P(None, ("group", "dom"), None),
        P(None, ("group", "dom"), None, None),
        P(None, ("group", "dom"), None),
        P(("group", "dom"), None),
        P("group", None),
    )
    out_specs = P(("group", "dom"), None, None, None)
    return jax.shard_map(shards, mesh=mesh, in_specs=in_specs, out_specs=out_specs, check_vma=False)
```

time: 92 us -> 80.9 us (0.88)
  blocking collectives: 0 us -> 25.7 us
  waiting for transfers between devices: 18.4 us -> 2.34 us
  starting transfers between devices: 43.7 us -> 34.3 us
  local copies, waits for them, and re-layouts: 8.58 us -> 0.75 us
  Pallas kernels: 18.8 us -> 17.2 us
  other arithmetic: 1.05 us -> 0 us
    all_to_all x0 -> x1, blocking collectives: none -> 25.7 us  [shards(): lax.all_to_all(packed, 'dom', split_axis=0, concat_axis=0, tiled=True)]
    all_to_all x1 -> x0, waiting for transfers between devices: 15.7 us -> none  [shards(): lax.all_to_all(packed, 'dom', split_axis=0, concat_axis=0, tiled=True)]
    all_to_all x1 -> x0, starting transfers between devices: 9.49 us -> none  [shards(): lax.all_to_all(packed, 'dom', split_axis=0, concat_axis=0, tiled=True)]
    unnamed x31 -> x26, local copies, waits for them, and re-layouts: 6.7 us -> 0.75 us
    pallas_call x6, Pallas kernels: 18.8 us -> 17.2 us  [call(): pl.pallas_call(lambda *refs: body(refs), out_shape=outs, in_specs=[pl.Blo...]
    reshape x7 -> x0, local copies, waits for them, and re-layouts: 1.61 us -> none  [the longest x2 1.15 us: shards(): star_table.reshape(kinds, -1)]
  transfers between devices with their start and end apart: 9 -> 8, of which waited for: 2 -> 1; matrix products, arithmetic and copies ran while one was open for 2% -> 0% of each run, Pallas kernels for 2% -> 4%
where the time goes in v1:
time: 80.9 us; the launch traced here: 80.5 us
  starting transfers between devices  34.3 us (42%)
  blocking collectives  25.7 us (32%)
  Pallas kernels  17.2 us (21%)
  waiting for transfers between devices  2.34 us (3%)
    ppermute x8, starting transfers between devices, exchange(): out += [lax.ppermute(higher, axis, up), lax.ppermute(lower, axis, down)]  34.3 us
    all_to_all x1, blocking collectives, shards(): lax.all_to_all(packed, 'dom', split_axis=0, concat_axis=0, tiled=True)  25.7 us
    pallas_call x6, Pallas kernels, call(): pl.pallas_call(lambda *refs: body(refs), out_shape=outs, in_specs=[pl.Blo...  17.2 us
    ppermute x8, waiting for transfers between devices, exchange(): out += [lax.ppermute(higher, axis, up), lax.ppermute(lower, axis, down)]  2.34 us
  transfers between devices with their start and end apart: 8, of which 1 were waited for; matrix products, arithmetic and copies ran while one was open for 0% of the time, Pallas kernels for 4%

profile of v1, /device:TPU:1, one launch (start us, length us, event | category | flops | bytes accessed | tf_op | source)
XLA Modules:
  0.0 80.5 jit_solution(10829364867256082593)
XLA Ops:
  0.0 0.0 copy-start.12
  0.0 0.0 copy-start.1
  0.0 0.0 copy-start.6
  0.0 0.0 copy-start.7
  0.0 6.2 %shard_map.145 = (f32[56,1152]{1,0:T(8,128)S(1)}, f32[4,216,128]{2,1,0:T(8,128)S(1)}, f32[112,128]{1,0:T(8,128)S(1)}, f32[112,128]{1,0:T(8,128)S(1)}, f32[112,12...) custom-call(f32[9,56,128]{2,1,0:T(8,128)} %bitcast.17, ...), custom_call_target="tpu_custom_call" | custom-call | tf_op jit(solution)/shard_map/pallas_call | solution.py:411
  6.2 0.0 copy-start
  6.2 4.2 %collective-permute-start = (f32[112,128]{1,0:T(8,128)S(1)}, f32[112,128]{1,0:T(8,128)S(1)}, u32[]{:S(2)}, u32[]{:S(2)}) collective-permute-start(f32[112,128]{1,0:T(8,128)S(1)} %get-tuple-element.40), channel_id=1, source_target_pairs={{0,32},{32,64},{64,96},{96,128},{128,160},{160,192},{192,224},{224... | collective-permute-start | bytes 172040 | tf_op jit(solution)/shard_map/ppermute | solution.py:427
  10.4 6.0 %collective-permute-start.1 = (f32[112,128]{1,0:T(8,128)S(1)}, f32[112,128]{1,0:T(8,128)S(1)}, u32[]{:S(2)}, u32[]{:S(2)}) collective-permute-start(f32[112,128]{1,0:T(8,128)S(1)} %get-tuple-element.41), channel_id=1, source_target_pairs={{32,0},{64,32},{96,64},{128,96},{160,128},{192,160},{224,192},{256... | collective-permute-start | bytes 172040 | tf_op jit(solution)/shard_map/ppermute | solution.py:427
  16.4 2.9 %collective-permute-start.2 = (f32[112,128]{1,0:T(8,128)S(1)}, f32[112,128]{1,0:T(8,128)S(1)}, u32[]{:S(2)}, u32[]{:S(2)}) collective-permute-start(f32[112,128]{1,0:T(8,128)S(1)} %get-tuple-element.42), channel_id=1, source_target_pairs={{0,1},{1,2},{2,3},{3,4},{4,5},{5,6},{6,7},{7,8},{8,9},{9,10},{10,1... | collective-permute-start | bytes 172040 | tf_op jit(solution)/shard_map/ppermute | solution.py:427
  19.4 10.4 %collective-permute-start.3 = (f32[112,128]{1,0:T(8,128)S(1)}, f32[112,128]{1,0:T(8,128)S(1)}, u32[]{:S(2)}, u32[]{:S(2)}) collective-permute-start(f32[112,128]{1,0:T(8,128)S(1)} %get-tuple-element.43), channel_id=1, source_target_pairs={{1,0},{2,1},{3,2},{4,3},{5,4},{6,5},{7,6},{8,7},{9,8},{10,9},{11,1... | collective-permute-start | bytes 172040 | tf_op jit(solution)/shard_map/ppermute | solution.py:427
  29.7 0.0 copy-done.12
  29.7 0.0 copy-start.3
  29.7 0.0 copy-start.5
  29.8 0.0 copy-start.4
  29.8 0.0 copy-start.10
  29.8 0.0 copy-start.11
  29.8 0.0 copy-done.1
  29.8 0.0 copy-done.6
  29.8 0.0 copy-done.7
  29.8 0.0 copy-done
  29.8 0.7 copy-done.3
  30.5 0.0 copy-done.8
  30.5 0.0 copy-done.5
  30.5 0.0 copy-done.4
  30.5 0.0 copy-done.10
  30.5 0.0 copy-done.11
  30.5 1.8 %shard_map.146 = (f32[56,1152]{1,0:T(8,128)S(1)}, f32[4,216,128]{2,1,0:T(8,128)S(1)}, f32[296,128]{1,0:T(8,128)S(1)}, f32[56,56]{1,0:T(8,128)S(1)}, f32[56,288]{1,0:T(8,128)S(1)}, /*index=5*/s32[2,128]{1,0:T(2,128)S(1)}) custom-call(f32[9,56,128]{2,1,0:T(8,128)S(1)} %bitcast.18, f32[56,1152]{1,0:T(8,128)S(1)} %get-tuple-element.34.refs_1_, ...), custom_call_target="tpu_custom_call" | custom-call | tf_op jit(solution)/shard_map/pallas_call | solution.py:411
  32.4 0.0 collective-permute-done.refs_2_
  32.4 0.0 collective-permute-done.1.refs_3_
  32.4 0.0 collective-permute-done.2.refs_4_
  32.4 0.0 collective-permute-done.3.refs_5_
  32.4 1.1 %shard_map.147 = (f32[56,1152]{1,0:T(8,128)S(1)}, f32[256,128]{1,0:T(8,128)S(1)}) custom-call(f32[56,1152]{1,0:T(8,128)S(1)} %get-tuple-element.38.refs_0_, f32[4,216,128]{2,1,0:T(8,128)S(1)} %get-tuple-element.39.refs_1_, f32[112,128]{1,0:T(8,128)S(1)} %collective-permute-done.refs_2_, f32[112,128]{1,0:T(8,128)S(1)} %collective-permute-done.1.refs_3_, ...), custom_call_target="tpu_custom_call" | custom-call | tf_op jit(solution)/shard_map/pallas_call | solution.py:411
  33.5 0.0 copy-start.2
  33.5 0.0 copy-start.9
  33.5 25.7 %all_to_all.11 = f32[32,8,128]{2,1,0:T(8,128)S(1)} all-to-all(f32[32,8,128]{2,1,0:T(8,128)S(1)} %bitcast.27), channel_id=1, replica_groups=mesh['group'=32,'dom'=32] {'dom'}, dimensions={0} | all-to-all | bytes 262144 | tf_op jit(solution)/shard_map/all_to_all | solution.py:492
  59.2 0.0 copy-done.2
  59.2 0.0 copy-done.9
  59.2 5.1 %shard_map.148 = (f32[56,1152]{1,0:T(8,128)S(1)}, f32[4,216,128]{2,1,0:T(8,128)S(1)}, f32[112,128]{1,0:T(8,128)S(1)}, f32[112,128]{1,0:T(8,128)S(1)}, f32[112,12...) custom-call(f32[56,1152]{1,0:T(8,128)S(1)} %get-tuple-element.48.ref, ...), custom_call_target="tpu_custom_call" | custom-call | tf_op jit(solution)/shard_map/pallas_call | solution.py:411
  64.3 1.9 %collective-permute-start.4 = (f32[112,128]{1,0:T(8,128)S(1)}, f32[112,128]{1,0:T(8,128)S(1)}, u32[]{:S(2)}, u32[]{:S(2)}) collective-permute-start(f32[112,128]{1,0:T(8,128)S(1)} %get-tuple-element.58), channel_id=1, source_target_pairs={{0,32},{32,64},{64,96},{96,128},{128,160},{160,192},{192,224},{224... | collective-permute-start | bytes 172040 | tf_op jit(solution)/shard_map/ppermute | solution.py:427
  66.2 6.7 %collective-permute-start.5 = (f32[112,128]{1,0:T(8,128)S(1)}, f32[112,128]{1,0:T(8,128)S(1)}, u32[]{:S(2)}, u32[]{:S(2)}) collective-permute-start(f32[112,128]{1,0:T(8,128)S(1)} %get-tuple-element.59), channel_id=1, source_target_pairs={{32,0},{64,32},{96,64},{128,96},{160,128},{192,160},{224,192},{256... | collective-permute-start | bytes 172040 | tf_op jit(solution)/shard_map/ppermute | solution.py:427
  72.9 2.1 %collective-permute-start.6 = (f32[112,128]{1,0:T(8,128)S(1)}, f32[112,128]{1,0:T(8,128)S(1)}, u32[]{:S(2)}, u32[]{:S(2)}) collective-permute-start(f32[112,128]{1,0:T(8,128)S(1)} %get-tuple-element.60), channel_id=1, source_target_pairs={{0,1},{1,2},{2,3},{3,4},{4,5},{5,6},{6,7},{7,8},{8,9},{9,10},{10,1... | collective-permute-start | bytes 172040 | tf_op jit(solution)/shard_map/ppermute | solution.py:427
  75.0 0.1 collective-permute-start.7
  75.1 1.4 %shard_map.149 = (f32[56,1152]{1,0:T(8,128)S(1)}, f32[4,216,128]{2,1,0:T(8,128)S(1)}, f32[296,128]{1,0:T(8,128)S(1)}) custom-call(f32[56,1152]{1,0:T(8,128)S(1)} %get-tuple-element.50.refs_0_, f32[56,1152]{1,0:T(8,128)S(1)} %get-tuple-element.51.refs_1_, f32[4,216,128]{2,1,0:T(8,128)S(1)} %get-tuple-element.52.refs_2_, ...), custom_call_target="tpu_custom_call" | custom-call | tf_op jit(solution)/shard_map/pallas_call | solution.py:411
  76.5 0.0 collective-permute-done.4.refs_2_
  76.5 0.0 collective-permute-done.5.refs_3_
  76.5 0.0 collective-permute-done.6.refs_4_
  76.5 2.3 %collective-permute-done.7.refs_5_ = f32[112,128]{1,0:T(8,128)S(1)} collective-permute-done((f32[112,128]{1,0:T(8,128)S(1)}, f32[112,128]{1,0:T(8,128)S(1)}, u32[]{:S(2)}, u32[]{:S(2)}) %collective-permute-start.7) | collective-permute-done | bytes 57376 | tf_op jit(solution)/shard_map/ppermute | solution.py:427
  78.9 1.6 %shard_map.150 = f32[9,56,128]{2,1,0:T(8,128)} custom-call(f32[56,1152]{1,0:T(8,128)S(1)} %get-tuple-element.56.refs_0_, f32[4,216,128]{2,1,0:T(8,128)S(1)} %get-tuple-element.57.refs_1_, f32[112,128]{1,0:T(8,128)S(1)} %collective-permute-done.4.refs_2_, f32[112,128]{1,0:T(8,128)S(1)} %collective-permute-done.5.refs_3_, ...), custom_call_target="tpu_custom_call" | custom-call | tf_op jit(solution)/shard_map/pallas_call | solution.py:411
  (2 shorter events, 0.0 us)
Async XLA Ops:
  0.0 29.7 %copy-start.12 = (f32[8,2,9,9]{3,1,2,0:T(2,128)S(1)}, f32[8,2,9,9]{3,1,2,0:T(2,128)}, u32[]{:S(2)}) copy-start(f32[8,2,9,9]{3,1,2,0:T(2,128)} %param.19) | copy-start | bytes 15556
  0.0 29.8 %copy-start.1 = (f32[1,56,9,128]{3,1,2,0:T(8,128)S(1)}, f32[1,56,9,128]{3,1,2,0:T(8,128)}, u32[]{:S(2)}) copy-start(f32[1,56,9,128]{3,1,2,0:T(8,128)} %param.15) | copy-start | bytes 774148
  0.0 29.8 %copy-start.6 = (f32[4,56,21]{1,0,2:T(4,128)S(1)}, f32[4,56,21]{1,0,2:T(4,128)}, u32[]{:S(2)}) copy-start(f32[4,56,21]{1,0,2:T(4,128)} %param.23) | copy-start | bytes 56452
  0.0 29.8 %copy-start.7 = (f32[3,21,21]{2,1,0:T(8,128)S(1)}, f32[3,21,21]{2,1,0:T(8,128)}, u32[]{:S(2)}) copy-start(f32[3,21,21]{2,1,0:T(8,128)} %refs_12_.1) | copy-start | bytes 15880
  6.2 23.6 %copy-start = (f32[3,56,56]{2,1,0:T(8,128)S(1)}, f32[3,56,56]{2,1,0:T(8,128)}, u32[]{:S(2)}) copy-start(f32[3,56,56]{2,1,0:T(8,128)} %refs_7_.6) | copy-start | bytes 112900
  6.2 26.1 %collective-permute-start = (f32[112,128]{1,0:T(8,128)S(1)}, f32[112,128]{1,0:T(8,128)S(1)}, u32[]{:S(2)}, u32[]{:S(2)}) collective-permute-start(f32[112,128]{1,0:T(8,128)S(1)} %get-tuple-element.40), channel_id=1, source_target_pairs={{0,32},{32,64},{64,96},{96,128},{128,160},{160,192},{192,224},{224... | collective-permute-start | bytes 172040 | tf_op jit(solution)/shard_map/ppermute | solution.py:427
  10.4 22.0 %collective-permute-start.1 = (f32[112,128]{1,0:T(8,128)S(1)}, f32[112,128]{1,0:T(8,128)S(1)}, u32[]{:S(2)}, u32[]{:S(2)}) collective-permute-start(f32[112,128]{1,0:T(8,128)S(1)} %get-tuple-element.41), channel_id=1, source_target_pairs={{32,0},{64,32},{96,64},{128,96},{160,128},{192,160},{224,192},{256... | collective-permute-start | bytes 172040 | tf_op jit(solution)/shard_map/ppermute | solution.py:427
  16.4 16.0 %collective-permute-start.2 = (f32[112,128]{1,0:T(8,128)S(1)}, f32[112,128]{1,0:T(8,128)S(1)}, u32[]{:S(2)}, u32[]{:S(2)}) collective-permute-start(f32[112,128]{1,0:T(8,128)S(1)} %get-tuple-element.42), channel_id=1, source_target_pairs={{0,1},{1,2},{2,3},{3,4},{4,5},{5,6},{6,7},{7,8},{8,9},{9,10},{10,1... | collective-permute-start | bytes 172040 | tf_op jit(solution)/shard_map/ppermute | solution.py:427
  19.4 13.0 %collective-permute-start.3 = (f32[112,128]{1,0:T(8,128)S(1)}, f32[112,128]{1,0:T(8,128)S(1)}, u32[]{:S(2)}, u32[]{:S(2)}) collective-permute-start(f32[112,128]{1,0:T(8,128)S(1)} %get-tuple-element.43), channel_id=1, source_target_pairs={{1,0},{2,1},{3,2},{4,3},{5,4},{6,5},{7,6},{8,7},{9,8},{10,9},{11,1... | collective-permute-start | bytes 172040 | tf_op jit(solution)/shard_map/ppermute | solution.py:427
  29.7 0.8 copy-start.3
  29.7 0.8 copy-start.8
  29.7 0.8 copy-start.5
  29.8 0.8 copy-start.4
  29.8 0.8 copy-start.10
  29.8 0.7 copy-start.11
  33.5 25.7 %copy-start.2 = (f32[8,3,9,9]{3,0,2,1:T(8,128)S(1)}, f32[8,3,9,9]{3,0,2,1:T(8,128)}, u32[]{:S(2)}) copy-start(f32[8,3,9,9]{3,0,2,1:T(8,128)} %param.18) | copy-start | bytes 23332
  33.5 25.7 %copy-start.9 = (s32[2,1,4,64]{3,2,1,0:T(4,128)S(1)}, s32[2,1,4,64]{3,2,1,0:T(4,128)}, u32[]{:S(2)}) copy-start(s32[2,1,4,64]{3,2,1,0:T(4,128)} %refs_5_.6) | copy-start | bytes 6148
  64.3 12.2 %collective-permute-start.4 = (f32[112,128]{1,0:T(8,128)S(1)}, f32[112,128]{1,0:T(8,128)S(1)}, u32[]{:S(2)}, u32[]{:S(2)}) collective-permute-start(f32[112,128]{1,0:T(8,128)S(1)} %get-tuple-element.58), channel_id=1, source_target_pairs={{0,32},{32,64},{64,96},{96,128},{128,160},{160,192},{192,224},{224... | collective-permute-start | bytes 172040 | tf_op jit(solution)/shard_map/ppermute | solution.py:427
  66.2 10.3 %collective-permute-start.5 = (f32[112,128]{1,0:T(8,128)S(1)}, f32[112,128]{1,0:T(8,128)S(1)}, u32[]{:S(2)}, u32[]{:S(2)}) collective-permute-start(f32[112,128]{1,0:T(8,128)S(1)} %get-tuple-element.59), channel_id=1, source_target_pairs={{32,0},{64,32},{96,64},{128,96},{160,128},{192,160},{224,192},{256... | collective-permute-start | bytes 172040 | tf_op jit(solution)/shard_map/ppermute | solution.py:427
  72.9 3.7 %collective-permute-start.6 = (f32[112,128]{1,0:T(8,128)S(1)}, f32[112,128]{1,0:T(8,128)S(1)}, u32[]{:S(2)}, u32[]{:S(2)}) collective-permute-start(f32[112,128]{1,0:T(8,128)S(1)} %get-tuple-element.60), channel_id=1, source_target_pairs={{0,1},{1,2},{2,3},{3,4},{4,5},{5,6},{6,7},{7,8},{8,9},{9,10},{10,1... | collective-permute-start | bytes 172040 | tf_op jit(solution)/shard_map/ppermute | solution.py:427
  75.0 3.9 %collective-permute-start.7 = (f32[112,128]{1,0:T(8,128)S(1)}, f32[112,128]{1,0:T(8,128)S(1)}, u32[]{:S(2)}, u32[]{:S(2)}) collective-permute-start(f32[112,128]{1,0:T(8,128)S(1)} %get-tuple-element.61), channel_id=1, source_target_pairs={{1,0},{2,1},{3,2},{4,3},{5,4},{6,5},{7,6},{8,7},{9,8},{10,9},{11,1... | collective-permute-start | bytes 172040 | tf_op jit(solution)/shard_map/ppermute | solution.py:427

commit v2 on v1

--- a/solution.py
+++ b/solution.py
@@ -13,6 +13,7 @@
 FACE_PAD = 24
 TRACE_ROWS = FIELDS * FACE_PAD
 MSG_ROWS = 112
+LATER = 7
 COEF_PAD = 16
 STAR_ROWS = 27 * COEF_PAD
 FLUX_ROWS = 18 * COEF_PAD
@@ -46,6 +47,16 @@
 
 def lane_gather(x, lane):
     return jnp.take_along_axis(x, jnp.broadcast_to(lane, x.shape), axis=1, mode="promise_in_bounds")
+
+
+def choose(traces, index):
+    rows, size = traces.shape
+    wide = (size, index.shape[1])
+    hot = (lax.broadcasted_iota(jnp.int32, wide, 0) == index).astype(bf16)
+    hi, lo = halves(traces)
+    return jnp.dot(hi, hot, preferred_element_type=f32) + jnp.dot(
+        lo, hot, preferred_element_type=f32
+    )
 
 
 def block(f):
@@ -110,8 +121,7 @@
     copies = [pltpu.make_async_copy(a, b, sems.at[n]) for n, (a, b) in enumerate(pairs)]
     for copy in copies:
         copy.start()
-    for copy in copies:
-        copy.wait()
+    return copies
 
 
 def one_hot(desc):
@@ -126,17 +136,16 @@
          integral_ref, trace_ref, m0, m1, m2, m3, ops_ref, hot_ref, placed_ref,
          wide_ref, deriv_ref, padded_ref) = refs
     else:
-        (state_in, geometry_in, material_in, star_in, send_in, stiff_in, project_in,
-         integral_ref, trace_ref, m0, m1, m2, m3, ops_ref, hot_ref, desc_ref,
-         wide_ref, deriv_ref, padded_ref,
-         state_ref, geometry_ref, material_ref, star_ref, send_ref, stiff_ref, project_ref,
-         sems) = refs
-        fetch(
-            [(state_in, state_ref), (geometry_in, geometry_ref), (material_in, material_ref),
-             (star_in, star_ref), (send_in, send_ref), (stiff_in, stiff_ref),
-             (project_in, project_ref)],
-            sems,
-        )
+        count = 7 + LATER
+        inputs, refs = refs[:count], refs[count:]
+        (integral_ref, trace_ref, m0, m1, m2, m3, ops_ref, hot_ref, desc_ref) = refs[:9]
+        held = refs[9 : 14 + LATER]
+        state_ref, star_ref, send_ref, stiff_ref, project_ref = held[:5]
+        (wide_ref, deriv_ref, padded_ref, geometry_ref, material_ref, sems) = refs[14 + LATER :]
+        targets = [geometry_ref, material_ref] + list(held)
+        copies = fetch(list(zip(inputs, targets)), sems)
+        for copy in copies[:7]:
+            copy.wait()
         desc_ref[...] = jnp.zeros((8, LANES), f32)
         for d in range(3):
             desc_ref[d : d + 1, :] = geometry_ref[d]
@@ -203,21 +212,18 @@
                     i * FACE_PAD : (i + 1) * FACE_PAD, block(t)
                 ]
 
-    low = lax.broadcasted_iota(jnp.int32, (8, LANES), 1) < 64
-    for c, msg_ref in enumerate((m0, m1, m2, m3)):
-        row = send_ref[phase, 0, c : c + 1, :]
-        index = jnp.broadcast_to(jnp.concatenate([row, row], axis=1), (8, LANES))
-        lane, face = index & 127, index >> 7
-        for r in range(MSG_ROWS // 8):
-            out = None
-            for i in range(4):
-                got = lane_gather(trace_ref[i, r * 8 : r * 8 + 8, :], lane)
-                high_row = r * 8 + MSG_ROWS
-                if high_row < TRACE_ROWS:
-                    other = lane_gather(trace_ref[i, high_row : high_row + 8, :], lane)
-                    got = jnp.where(low, got, other)
-                out = got if out is None else jnp.where(face == i, got, out)
-            msg_ref[r * 8 : r * 8 + 8, :] = out
+    traces = jnp.concatenate([trace_ref[i] for i in range(4)], axis=1)
+    low = lax.broadcasted_iota(jnp.int32, (MSG_ROWS, LANES), 1) < 64
+    fill = jnp.zeros((2 * MSG_ROWS - TRACE_ROWS, LANES), f32)
+    for k, (a, b) in enumerate(((m0, m1), (m2, m3))):
+        pair = [send_ref[phase, 0, c : c + 1, :] for c in (2 * k, 2 * k + 1)]
+        sent = choose(traces, jnp.concatenate(pair, axis=1))
+        upper = jnp.concatenate([sent[MSG_ROWS:], fill], axis=0)
+        a[...] = jnp.where(low, sent[:MSG_ROWS], pltpu.roll(upper, 64, 1))
+        b[...] = jnp.where(low, pltpu.roll(sent[:MSG_ROWS], 64, 1), upper)
+    if not place:
+        for copy in copies[7:]:
+            copy.wait()
 
 
 def to_column(row, size):
@@ -403,10 +409,7 @@
 
 def call(body, outs, scratch, *args, raw=False):
     space = pltpu.HBM if raw else pltpu.VMEM
-    scratch = [pltpu.VMEM(s, f32) for s in scratch]
-    if raw:
-        scratch += [pltpu.VMEM(a.shape, a.dtype) for a in args]
-        scratch += [pltpu.SemaphoreType.DMA((len(args),))]
+    scratch = [s if not isinstance(s, tuple) else pltpu.VMEM(s, f32) for s in scratch]
     outs = [s if isinstance(s, jax.ShapeDtypeStruct) else jax.ShapeDtypeStruct(s, f32) for s in outs]
     return pl.pallas_call(
         lambda *refs: body(refs),
@@ -468,47 +471,54 @@
     maps_shape = jax.ShapeDtypeStruct((2, LANES), jnp.int32)
     first_scratch = [wide, (2,) + full, (4 * FACE_PAD, modes)]
 
-    integral, trace, a, b, c, d, ops, hot, desc = call(
+    kept = [state, star, send_faces, stiffness, face_project,
+            face_lift, reorient, leaving_slots, leaving_owner, neighbour_face, orientation, cohesion]
+    (integral, trace, a, b, c, d, ops, hot, desc,
+     state, star, sends, stiff, project, *later) = call(
         functools.partial(first_half_body, False),
-        [full, traces, msg, msg, msg, msg, ops_shape, tile, tile],
-        first_scratch,
-        state, geometry, material, star, send_faces, stiffness, face_project,
+        [full, traces, msg, msg, msg, msg, ops_shape, tile, tile]
+        + [jax.ShapeDtypeStruct(a.shape, a.dtype) for a in kept],
+        first_scratch
+        + [pltpu.VMEM(geometry.shape, f32), pltpu.VMEM(material.shape, jnp.int32),
+           pltpu.SemaphoreType.DMA((2 + len(kept),))],
+        geometry, material, *kept,
         raw=True,
     )
+    face_lift, reorient, slots, owners, near, orient, cohesion = later
     incoming = exchange([a, b, c, d])
     partial, local, flux_rows, own, lift, maps = call(
         functools.partial(middle_body, 0),
         [full, traces, flux_shape, (modes, modes), lift_shape, maps_shape],
         [wide_more, (12 * FACE_PAD, modes)],
-        state, integral, trace, ops, hot, neighbour_face, orientation, stiffness, flux, cohesion,
-        face_lift, face_project, reorient, leaving_slots, leaving_owner,
+        state, integral, trace, ops, hot, near, orient, stiff, flux, cohesion,
+        face_lift, project, reorient, slots, owners,
     )
     stepped, packed = call(
         functools.partial(last_half_body, True),
         [full, (256, LANES)],
         [wide_flux, (2,) + traces[1:], traces, full],
-        partial, local, *incoming, flux_rows, neighbour_face, orientation, lift, desc, maps,
+        partial, local, *incoming, flux_rows, near, orient, lift, desc, maps,
     )
     moved = lax.all_to_all(packed, "dom", split_axis=0, concat_axis=0, tiled=True)
     integral, trace, a, b, c, d, ops, hot, placed = call(
         functools.partial(first_half_body, True),
         [full, traces, msg, msg, msg, msg, ops_shape, tile, full],
         first_scratch,
-        stepped, moved, maps, desc, star, send_faces, stiffness, face_project,
+        stepped, moved, maps, desc, star, sends, stiff, project,
     )
     incoming = exchange([a, b, c, d])
     partial, local, flux_rows = call(
         functools.partial(middle_body, 1),
         [full, traces, flux_shape],
         [wide_more],
-        placed, integral, trace, ops, hot, neighbour_face, orientation, stiffness, flux,
+        placed, integral, trace, ops, hot, near, orient, stiff, flux,
         cohesion, own,
     )
     (final,) = call(
         functools.partial(last_half_body, False),
         [(nfield, modes, elem_count)],
         [wide_flux, (2,) + traces[1:], traces, full],
-        partial, local, *incoming, flux_rows, neighbour_face, orientation, lift,
+        partial, local, *incoming, flux_rows, near, orient, lift,
     )
     return jnp.transpose(final, (1, 0, 2))[None]
 

time: 80.9 us -> 79.7 us (0.985)
  no operation moved by 1% of the time
where the time goes in v2:
time: 79.7 us; the launch traced here: 79.4 us
  starting transfers between devices  34.2 us (43%)
  blocking collectives  26.4 us (33%)
  Pallas kernels  16.4 us (21%)
  waiting for transfers between devices  2.34 us (3%)
    ppermute x8, starting transfers between devices, exchange(): out += [lax.ppermute(higher, axis, up), lax.ppermute(lower, axis, down)]  34.2 us
    all_to_all x1, blocking collectives, shards(): lax.all_to_all(packed, 'dom', split_axis=0, concat_axis=0, tiled=True)  26.4 us
    pallas_call x6, Pallas kernels, call(): pl.pallas_call(lambda *refs: body(refs), out_shape=outs, in_specs=[pl.Blo...  16.4 us
    ppermute x8, waiting for transfers between devices, exchange(): out += [lax.ppermute(higher, axis, up), lax.ppermute(lower, axis, down)]  2.34 us
  transfers between devices with their start and end apart: 8, of which 1 were waited for; matrix products, arithmetic and copies ran while one was open for 0% of the time, Pallas kernels for 4%

profile of v2, /device:TPU:1, one launch (start us, length us, event | category | flops | bytes accessed | tf_op | source)
XLA Modules:
  0.0 79.4 jit_solution(10619415103696845809)
XLA Ops:
  0.0 0.0 copy-start
  0.0 5.9 %shard_map.145 = (f32[56,1152]{1,0:T(8,128)S(1)}, f32[4,216,128]{2,1,0:T(8,128)S(1)}, f32[112,128]{1,0:T(8,128)S(1)}, f32[112,128]{1,0:T(8,128)S(1)}, f32[112,12...) custom-call(f32[3,1,128]{2,1,0:T(1,128)} %bitcast.26, ...), custom_call_target="tpu_custom_call" | custom-call | tf_op jit(solution)/shard_map/pallas_call | solution.py:414
  5.9 4.0 %collective-permute-start = (f32[112,128]{1,0:T(8,128)S(1)}, f32[112,128]{1,0:T(8,128)S(1)}, u32[]{:S(2)}, u32[]{:S(2)}) collective-permute-start(f32[112,128]{1,0:T(8,128)S(1)} %get-tuple-element.62), channel_id=1, source_target_pairs={{0,32},{32,64},{64,96},{96,128},{128,160},{160,192},{192,224},{224... | collective-permute-start | bytes 172040 | tf_op jit(solution)/shard_map/ppermute | solution.py:430
  9.9 6.0 %collective-permute-start.1 = (f32[112,128]{1,0:T(8,128)S(1)}, f32[112,128]{1,0:T(8,128)S(1)}, u32[]{:S(2)}, u32[]{:S(2)}) collective-permute-start(f32[112,128]{1,0:T(8,128)S(1)} %get-tuple-element.63), channel_id=1, source_target_pairs={{32,0},{64,32},{96,64},{128,96},{160,128},{192,160},{224,192},{256... | collective-permute-start | bytes 172040 | tf_op jit(solution)/shard_map/ppermute | solution.py:430
  15.9 2.9 %collective-permute-start.2 = (f32[112,128]{1,0:T(8,128)S(1)}, f32[112,128]{1,0:T(8,128)S(1)}, u32[]{:S(2)}, u32[]{:S(2)}) collective-permute-start(f32[112,128]{1,0:T(8,128)S(1)} %get-tuple-element.64), channel_id=1, source_target_pairs={{0,1},{1,2},{2,3},{3,4},{4,5},{5,6},{6,7},{7,8},{8,9},{9,10},{10,1... | collective-permute-start | bytes 172040 | tf_op jit(solution)/shard_map/ppermute | solution.py:430
  18.9 10.4 %collective-permute-start.3 = (f32[112,128]{1,0:T(8,128)S(1)}, f32[112,128]{1,0:T(8,128)S(1)}, u32[]{:S(2)}, u32[]{:S(2)}) collective-permute-start(f32[112,128]{1,0:T(8,128)S(1)} %get-tuple-element.65), channel_id=1, source_target_pairs={{1,0},{2,1},{3,2},{4,3},{5,4},{6,5},{7,6},{8,7},{9,8},{10,9},{11,1... | collective-permute-start | bytes 172040 | tf_op jit(solution)/shard_map/ppermute | solution.py:430
  29.2 0.0 copy-done
  29.2 1.8 %shard_map.146 = (f32[56,1152]{1,0:T(8,128)S(1)}, f32[4,216,128]{2,1,0:T(8,128)S(1)}, f32[296,128]{1,0:T(8,128)S(1)}, f32[56,56]{1,0:T(8,128)S(1)}, f32[56,288]{1,0:T(8,128)S(1)}, /*index=5*/s32[2,128]{1,0:T(2,128)S(1)}) custom-call(f32[9,56,128]{2,1,0:T(8,128)S(1)} %get-tuple-element.46.refs_0_, f32[56,1152]{1,0:T(8,128)S(1)} %get-tuple-element.47.refs_1_, ...), custom_call_target="tpu_custom_call" | custom-call | tf_op jit(solution)/shard_map/pallas_call | solution.py:414
  31.1 0.0 collective-permute-done.refs_2_
  31.1 0.0 collective-permute-done.1.refs_3_
  31.1 0.0 collective-permute-done.2.refs_4_
  31.1 0.0 collective-permute-done.3.refs_5_
  31.1 1.1 %shard_map.147 = (f32[56,1152]{1,0:T(8,128)S(1)}, f32[256,128]{1,0:T(8,128)S(1)}) custom-call(f32[56,1152]{1,0:T(8,128)S(1)} %get-tuple-element.60.refs_0_, f32[4,216,128]{2,1,0:T(8,128)S(1)} %get-tuple-element.61.refs_1_, f32[112,128]{1,0:T(8,128)S(1)} %collective-permute-done.refs_2_, f32[112,128]{1,0:T(8,128)S(1)} %collective-permute-done.1.refs_3_, ...), custom_call_target="tpu_custom_call" | custom-call | tf_op jit(solution)/shard_map/pallas_call | solution.py:414
  32.2 26.4 %all_to_all.11 = f32[32,8,128]{2,1,0:T(8,128)S(1)} all-to-all(f32[32,8,128]{2,1,0:T(8,128)S(1)} %bitcast.20), channel_id=1, replica_groups=mesh['group'=32,'dom'=32] {'dom'}, dimensions={0} | all-to-all | bytes 262144 | tf_op jit(solution)/shard_map/all_to_all | solution.py:502
  58.5 4.6 %shard_map.148 = (f32[56,1152]{1,0:T(8,128)S(1)}, f32[4,216,128]{2,1,0:T(8,128)S(1)}, f32[112,128]{1,0:T(8,128)S(1)}, f32[112,128]{1,0:T(8,128)S(1)}, f32[112,12...) custom-call(f32[56,1152]{1,0:T(8,128)S(1)} %get-tuple-element.70.ref, ...), custom_call_target="tpu_custom_call" | custom-call | tf_op jit(solution)/shard_map/pallas_call | solution.py:414
  63.2 1.9 %collective-permute-start.4 = (f32[112,128]{1,0:T(8,128)S(1)}, f32[112,128]{1,0:T(8,128)S(1)}, u32[]{:S(2)}, u32[]{:S(2)}) collective-permute-start(f32[112,128]{1,0:T(8,128)S(1)} %get-tuple-element.82), channel_id=1, source_target_pairs={{0,32},{32,64},{64,96},{96,128},{128,160},{160,192},{192,224},{224... | collective-permute-start | bytes 172040 | tf_op jit(solution)/shard_map/ppermute | solution.py:430
  65.1 6.7 %collective-permute-start.5 = (f32[112,128]{1,0:T(8,128)S(1)}, f32[112,128]{1,0:T(8,128)S(1)}, u32[]{:S(2)}, u32[]{:S(2)}) collective-permute-start(f32[112,128]{1,0:T(8,128)S(1)} %get-tuple-element.83), channel_id=1, source_target_pairs={{32,0},{64,32},{96,64},{128,96},{160,128},{192,160},{224,192},{256... | collective-permute-start | bytes 172040 | tf_op jit(solution)/shard_map/ppermute | solution.py:430
  71.8 2.1 %collective-permute-start.6 = (f32[112,128]{1,0:T(8,128)S(1)}, f32[112,128]{1,0:T(8,128)S(1)}, u32[]{:S(2)}, u32[]{:S(2)}) collective-permute-start(f32[112,128]{1,0:T(8,128)S(1)} %get-tuple-element.84), channel_id=1, source_target_pairs={{0,1},{1,2},{2,3},{3,4},{4,5},{5,6},{6,7},{7,8},{8,9},{9,10},{10,1... | collective-permute-start | bytes 172040 | tf_op jit(solution)/shard_map/ppermute | solution.py:430
  73.9 0.1 collective-permute-start.7
  74.0 1.4 %shard_map.149 = (f32[56,1152]{1,0:T(8,128)S(1)}, f32[4,216,128]{2,1,0:T(8,128)S(1)}, f32[296,128]{1,0:T(8,128)S(1)}) custom-call(f32[56,1152]{1,0:T(8,128)S(1)} %get-tuple-element.74.refs_0_, f32[56,1152]{1,0:T(8,128)S(1)} %get-tuple-element.75.refs_1_, f32[4,216,128]{2,1,0:T(8,128)S(1)} %get-tuple-element.76.refs_2_, ...), custom_call_target="tpu_custom_call" | custom-call | tf_op jit(solution)/shard_map/pallas_call | solution.py:414
  75.4 0.0 collective-permute-done.4.refs_2_
  75.4 0.0 collective-permute-done.5.refs_3_
  75.5 0.0 collective-permute-done.6.refs_4_
  75.5 2.3 %collective-permute-done.7.refs_5_ = f32[112,128]{1,0:T(8,128)S(1)} collective-permute-done((f32[112,128]{1,0:T(8,128)S(1)}, f32[112,128]{1,0:T(8,128)S(1)}, u32[]{:S(2)}, u32[]{:S(2)}) %collective-permute-start.7) | collective-permute-done | bytes 57376 | tf_op jit(solution)/shard_map/ppermute | solution.py:430
  77.8 1.6 %shard_map.150 = f32[9,56,128]{2,1,0:T(8,128)} custom-call(f32[56,1152]{1,0:T(8,128)S(1)} %get-tuple-element.80.refs_0_, f32[4,216,128]{2,1,0:T(8,128)S(1)} %get-tuple-element.81.refs_1_, f32[112,128]{1,0:T(8,128)S(1)} %collective-permute-done.4.refs_2_, f32[112,128]{1,0:T(8,128)S(1)} %collective-permute-done.5.refs_3_, ...), custom_call_target="tpu_custom_call" | custom-call | tf_op jit(solution)/shard_map/pallas_call | solution.py:414
  (1 shorter events, 0.0 us)
Async XLA Ops:
  0.0 29.2 %copy-start = (f32[8,2,9,9]{3,1,2,0:T(2,128)S(1)}, f32[8,2,9,9]{3,1,2,0:T(2,128)}, u32[]{:S(2)}) copy-start(f32[8,2,9,9]{3,1,2,0:T(2,128)} %param.19) | copy-start | bytes 15556
  5.9 25.2 %collective-permute-start = (f32[112,128]{1,0:T(8,128)S(1)}, f32[112,128]{1,0:T(8,128)S(1)}, u32[]{:S(2)}, u32[]{:S(2)}) collective-permute-start(f32[112,128]{1,0:T(8,128)S(1)} %get-tuple-element.62), channel_id=1, source_target_pairs={{0,32},{32,64},{64,96},{96,128},{128,160},{160,192},{192,224},{224... | collective-permute-start | bytes 172040 | tf_op jit(solution)/shard_map/ppermute | solution.py:430
  9.9 21.2 %collective-permute-start.1 = (f32[112,128]{1,0:T(8,128)S(1)}, f32[112,128]{1,0:T(8,128)S(1)}, u32[]{:S(2)}, u32[]{:S(2)}) collective-permute-start(f32[112,128]{1,0:T(8,128)S(1)} %get-tuple-element.63), channel_id=1, source_target_pairs={{32,0},{64,32},{96,64},{128,96},{160,128},{192,160},{224,192},{256... | collective-permute-start | bytes 172040 | tf_op jit(solution)/shard_map/ppermute | solution.py:430
  15.9 15.2 %collective-permute-start.2 = (f32[112,128]{1,0:T(8,128)S(1)}, f32[112,128]{1,0:T(8,128)S(1)}, u32[]{:S(2)}, u32[]{:S(2)}) collective-permute-start(f32[112,128]{1,0:T(8,128)S(1)} %get-tuple-element.64), channel_id=1, source_target_pairs={{0,1},{1,2},{2,3},{3,4},{4,5},{5,6},{6,7},{7,8},{8,9},{9,10},{10,1... | collective-permute-start | bytes 172040 | tf_op jit(solution)/shard_map/ppermute | solution.py:430
  18.9 12.2 %collective-permute-start.3 = (f32[112,128]{1,0:T(8,128)S(1)}, f32[112,128]{1,0:T(8,128)S(1)}, u32[]{:S(2)}, u32[]{:S(2)}) collective-permute-start(f32[112,128]{1,0:T(8,128)S(1)} %get-tuple-element.65), channel_id=1, source_target_pairs={{1,0},{2,1},{3,2},{4,3},{5,4},{6,5},{7,6},{8,7},{9,8},{10,9},{11,1... | collective-permute-start | bytes 172040 | tf_op jit(solution)/shard_map/ppermute | solution.py:430
  63.2 12.3 %collective-permute-start.4 = (f32[112,128]{1,0:T(8,128)S(1)}, f32[112,128]{1,0:T(8,128)S(1)}, u32[]{:S(2)}, u32[]{:S(2)}) collective-permute-start(f32[112,128]{1,0:T(8,128)S(1)} %get-tuple-element.82), channel_id=1, source_target_pairs={{0,32},{32,64},{64,96},{96,128},{128,160},{160,192},{192,224},{224... | collective-permute-start | bytes 172040 | tf_op jit(solution)/shard_map/ppermute | solution.py:430
  65.1 10.3 %collective-permute-start.5 = (f32[112,128]{1,0:T(8,128)S(1)}, f32[112,128]{1,0:T(8,128)S(1)}, u32[]{:S(2)}, u32[]{:S(2)}) collective-permute-start(f32[112,128]{1,0:T(8,128)S(1)} %get-tuple-element.83), channel_id=1, source_target_pairs={{32,0},{64,32},{96,64},{128,96},{160,128},{192,160},{224,192},{256... | collective-permute-start | bytes 172040 | tf_op jit(solution)/shard_map/ppermute | solution.py:430
  71.8 3.7 %collective-permute-start.6 = (f32[112,128]{1,0:T(8,128)S(1)}, f32[112,128]{1,0:T(8,128)S(1)}, u32[]{:S(2)}, u32[]{:S(2)}) collective-permute-start(f32[112,128]{1,0:T(8,128)S(1)} %get-tuple-element.84), channel_id=1, source_target_pairs={{0,1},{1,2},{2,3},{3,4},{4,5},{5,6},{6,7},{7,8},{8,9},{9,10},{10,1... | collective-permute-start | bytes 172040 | tf_op jit(solution)/shard_map/ppermute | solution.py:430
  73.9 3.9 %collective-permute-start.7 = (f32[112,128]{1,0:T(8,128)S(1)}, f32[112,128]{1,0:T(8,128)S(1)}, u32[]{:S(2)}, u32[]{:S(2)}) collective-permute-start(f32[112,128]{1,0:T(8,128)S(1)} %get-tuple-element.85), channel_id=1, source_target_pairs={{1,0},{2,1},{3,2},{4,3},{5,4},{6,5},{7,6},{8,7},{9,8},{10,9},{11,1... | collective-permute-start | bytes 172040 | tf_op jit(solution)/shard_map/ppermute | solution.py:430

commit v3 on v2

--- a/solution.py
+++ b/solution.py
@@ -87,21 +87,15 @@
     return exact_dot(jnp.where(pair == at, stacked, 0.0), many)
 
 
-def spread_rows(ops_ref, first, count, wide_ref, start=0):
-    for p in range(count):
-        for g in range(FIELDS):
-            r = (first + p) * COEF_PAD + g
-            wide_ref[start + p * FIELDS + g] = jnp.broadcast_to(ops_ref[r : r + 1, :], (8, LANES))
-
-
-def mix(load, wide_ref, start, outs):
+def mix(load, rows_ref, start, outs):
     accs = [None] * len(outs)
     for f in range(FIELDS):
         value = load(f)
         rows = value.shape[0]
         value = value.reshape(rows // 8, 8, LANES)
         for t, g in enumerate(outs):
-            part = value * wide_ref[start + f * FIELDS + g][None]
+            r = (start // FIELDS + f) * COEF_PAD + g
+            part = value * jnp.broadcast_to(rows_ref[r : r + 1, :], (8, LANES))[None]
             accs[t] = part if accs[t] is None else accs[t] + part
     return [a.reshape(-1, LANES) for a in accs]
 
@@ -109,11 +103,11 @@
 GROUPS_OF_FIELDS = ((0, 1), (2, 3), (4, 5), (6, 7), (8,))
 
 
-def star_mixed(src_ref, wide_ref, outs):
+def star_mixed(src_ref, rows_ref, outs):
     load = lambda f: src_ref[:, block(f)]
     parts = []
     for d in range(3):
-        parts.append(jnp.concatenate(mix(load, wide_ref, d * 81, outs), axis=1))
+        parts.append(jnp.concatenate(mix(load, rows_ref, d * 81, outs), axis=1))
     return jnp.concatenate(parts, axis=0)
 
 
@@ -134,14 +128,14 @@
     if place:
         (state_ref, recv_ref, maps_ref, desc_ref, star_ref, send_ref, stiff_ref, project_ref,
          integral_ref, trace_ref, m0, m1, m2, m3, ops_ref, hot_ref, placed_ref,
-         wide_ref, deriv_ref, padded_ref) = refs
+         deriv_ref, padded_ref) = refs
     else:
         count = 7 + LATER
         inputs, refs = refs[:count], refs[count:]
         (integral_ref, trace_ref, m0, m1, m2, m3, ops_ref, hot_ref, desc_ref) = refs[:9]
         held = refs[9 : 14 + LATER]
         state_ref, star_ref, send_ref, stiff_ref, project_ref = held[:5]
-        (wide_ref, deriv_ref, padded_ref, geometry_ref, material_ref, sems) = refs[14 + LATER :]
+        (deriv_ref, padded_ref, geometry_ref, material_ref, sems) = refs[14 + LATER :]
         targets = [geometry_ref, material_ref] + list(held)
         copies = fetch(list(zip(inputs, targets)), sems)
         for copy in copies[:7]:
@@ -179,8 +173,6 @@
     third = STAR_ROWS // 3
     scale = jnp.where(row_at < third, desc[0:1], jnp.where(row_at < 2 * third, desc[1:2], desc[2:3]))
     ops_ref[...] = rows * scale
-    spread_rows(ops_ref, 0, 27, wide_ref)
-
     across = jnp.concatenate([jnp.transpose(stiff_ref[d], (1, 0)) for d in range(3)], axis=0)
     stiff = left_matrix(-jnp.transpose(across, (1, 0)))
     deriv_ref[0] = integral_ref[...]
@@ -189,7 +181,7 @@
         now = deriv_ref.at[j % 2]
         later = deriv_ref.at[(j + 1) % 2]
         for outs in GROUPS_OF_FIELDS:
-            new = mm(stiff, star_mixed(now, wide_ref, outs))
+            new = mm(stiff, star_mixed(now, ops_ref, outs))
             lanes = slice(outs[0] * LANES, (outs[-1] + 1) * LANES)
             later[:, lanes] = new
             integral_ref[:, lanes] = integral_ref[:, lanes] + new * coef
@@ -279,7 +271,7 @@
     if phase == 0:
         (lift_in, project_ref, reorient_ref, slots_ref, owners_ref,
          partial_ref, local_ref, flux_rows_ref, own_ref, lift_ref, maps_ref,
-         wide_ref, columns_ref) = refs[10:]
+         columns_ref) = refs[10:]
         own_ref[...] = sum(
             jnp.dot(
                 jnp.transpose(lift_in[:, i, :], (1, 0)), project_ref[:, i, :],
@@ -301,21 +293,19 @@
         maps_ref[0:1, :] = source
         maps_ref[1:2, :] = arriving
     else:
-        own_ref, partial_ref, local_ref, flux_rows_ref, wide_ref = refs[10:]
+        own_ref, partial_ref, local_ref, flux_rows_ref = refs[10:]
     modes = stiff_ref.shape[1]
     hot = hot_ref[...]
     flux_rows_ref[0:FLUX_ROWS, :] = coefficient_rows(flux_ref[...], hot)
     yield_rows = exact_dot(jnp.broadcast_to(cohesion_ref[...], (8, 8)), hot.astype(bf16))
     flux_rows_ref[FLUX_ROWS : FLUX_ROWS + 8, :] = yield_rows
-    spread_rows(ops_ref, 0, 27, wide_ref)
-    spread_rows(flux_rows_ref, 0, 9, wide_ref, 243)
     volume = left_matrix(jnp.transpose(stiff_ref[...].reshape(3 * modes, modes), (1, 0)))
     own = left_matrix(own_ref[...])
     for outs in GROUPS_OF_FIELDS:
         lanes = slice(outs[0] * LANES, (outs[-1] + 1) * LANES)
         load = lambda f: integral_ref[:, block(f)]
-        added = mm(volume, star_mixed(integral_ref, wide_ref, outs))
-        flux = mm(own, jnp.concatenate(mix(load, wide_ref, 243, outs), axis=1))
+        added = mm(volume, star_mixed(integral_ref, ops_ref, outs))
+        flux = mm(own, jnp.concatenate(mix(load, flux_rows_ref, 0, outs), axis=1))
         if len(state_ref.shape) == 3:
             before = jnp.concatenate([state_ref[g] for g in outs], axis=1)
         else:
@@ -337,12 +327,11 @@
     phase = 0 if pack else 1
     if pack:
         (partial_ref, local_ref, m0, m1, m2, m3, ops_ref, near_ref, orient_ref, lift_ref,
-         desc_ref, maps_ref, out_ref, packed_ref, wide_ref, both_ref, turned_ref, sum_ref) = refs
+         desc_ref, maps_ref, out_ref, packed_ref, both_ref, turned_ref, sum_ref) = refs
     else:
         (partial_ref, local_ref, m0, m1, m2, m3, ops_ref, near_ref, orient_ref, lift_ref,
-         out_ref, wide_ref, both_ref, turned_ref, sum_ref) = refs
+         out_ref, both_ref, turned_ref, sum_ref) = refs
     modes = lift_ref.shape[0]
-    spread_rows(ops_ref, 9, 9, wide_ref)
 
     low = lax.broadcasted_iota(jnp.int32, (MSG_ROWS, LANES), 1) < 64
     rest = TRACE_ROWS - MSG_ROWS
@@ -368,7 +357,7 @@
         pieces = []
         for i in range(4):
             load = lambda f: turned_ref[i, f * FACE_PAD : (f + 1) * FACE_PAD, :]
-            mixed = mix(load, wide_ref, 0, outs)
+            mixed = mix(load, ops_ref, 81, outs)
             orient = jnp.broadcast_to(orient_ref[phase, :, block(i)], (FACE_PAD, LANES))
             for h in range(3):
                 pieces.append(
@@ -464,12 +453,9 @@
     tile = (8, LANES)
     ops_shape = (STAR_ROWS, LANES)
     flux_shape = (FLUX_ROWS + 8, LANES)
-    wide = (243, 8, LANES)
-    wide_more = (324, 8, LANES)
-    wide_flux = (81, 8, LANES)
     lift_shape = (modes, 12 * FACE_PAD)
     maps_shape = jax.ShapeDtypeStruct((2, LANES), jnp.int32)
-    first_scratch = [wide, (2,) + full, (4 * FACE_PAD, modes)]
+    first_scratch = [(2,) + full, (4 * FACE_PAD, modes)]
 
     kept = [state, star, send_faces, stiffness, face_project,
             face_lift, reorient, leaving_slots, leaving_owner, neighbour_face, orientation, cohesion]
@@ -489,14 +475,14 @@
     partial, local, flux_rows, own, lift, maps = call(
         functools.partial(middle_body, 0),
         [full, traces, flux_shape, (modes, modes), lift_shape, maps_shape],
-        [wide_more, (12 * FACE_PAD, modes)],
+        [(12 * FACE_PAD, modes)],
         state, integral, trace, ops, hot, near, orient, stiff, flux, cohesion,
         face_lift, project, reorient, slots, owners,
     )
     stepped, packed = call(
         functools.partial(last_half_body, True),
         [full, (256, LANES)],
-        [wide_flux, (2,) + traces[1:], traces, full],
+        [(2,) + traces[1:], traces, full],
         partial, local, *incoming, flux_rows, near, orient, lift, desc, maps,
     )
     moved = lax.all_to_all(packed, "dom", split_axis=0, concat_axis=0, tiled=True)
@@ -510,14 +496,14 @@
     partial, local, flux_rows = call(
         functools.partial(middle_body, 1),
         [full, traces, flux_shape],
-        [wide_more],
+        [],
         placed, integral, trace, ops, hot, near, orient, stiff, flux,
         cohesion, own,
     )
     (final,) = call(
         functools.partial(last_half_body, False),
         [(nfield, modes, elem_count)],
-        [wide_flux, (2,) + traces[1:], traces, full],
+        [(2,) + traces[1:], traces, full],
         partial, local, *incoming, flux_rows, near, orient, lift,
     )
     return jnp.transpose(final, (1, 0, 2))[None]

time: 79.7 us -> 79.7 us (level)
  no operation moved by 1% of the time
where the time goes in v3:
time: 79.7 us; the launch traced here: 79.4 us
  starting transfers between devices  34.2 us (43%)
  blocking collectives  26.4 us (33%)
  Pallas kernels  16.4 us (21%)
  waiting for transfers between devices  2.35 us (3%)
    ppermute x8, starting transfers between devices, exchange(): out += [lax.ppermute(higher, axis, up), lax.ppermute(lower, axis, down)]  34.2 us
    all_to_all x1, blocking collectives, shards(): lax.all_to_all(packed, 'dom', split_axis=0, concat_axis=0, tiled=True)  26.4 us
    pallas_call x6, Pallas kernels, call(): pl.pallas_call(lambda *refs: body(refs), out_shape=outs, in_specs=[pl.Blo...  16.4 us
    ppermute x8, waiting for transfers between devices, exchange(): out += [lax.ppermute(higher, axis, up), lax.ppermute(lower, axis, down)]  2.35 us
  transfers between devices with their start and end apart: 8, of which 1 were waited for; matrix products, arithmetic and copies ran while one was open for 0% of the time, Pallas kernels for 4%

profile of v3, /device:TPU:1, one launch (start us, length us, event | category | flops | bytes accessed | tf_op | source)
XLA Modules:
  0.0 79.4 jit_solution(7350093144724060623)
XLA Ops:
  0.0 0.0 copy-start
  0.0 5.9 %shard_map.145 = (f32[56,1152]{1,0:T(8,128)S(1)}, f32[4,216,128]{2,1,0:T(8,128)S(1)}, f32[112,128]{1,0:T(8,128)S(1)}, f32[112,128]{1,0:T(8,128)S(1)}, f32[112,12...) custom-call(f32[3,1,128]{2,1,0:T(1,128)} %bitcast.26, ...), custom_call_target="tpu_custom_call" | custom-call | tf_op jit(solution)/shard_map/pallas_call | solution.py:403
  5.9 4.0 %collective-permute-start = (f32[112,128]{1,0:T(8,128)S(1)}, f32[112,128]{1,0:T(8,128)S(1)}, u32[]{:S(2)}, u32[]{:S(2)}) collective-permute-start(f32[112,128]{1,0:T(8,128)S(1)} %get-tuple-element.62), channel_id=1, source_target_pairs={{0,32},{32,64},{64,96},{96,128},{128,160},{160,192},{192,224},{224... | collective-permute-start | bytes 172040 | tf_op jit(solution)/shard_map/ppermute | solution.py:419
  9.9 6.0 %collective-permute-start.1 = (f32[112,128]{1,0:T(8,128)S(1)}, f32[112,128]{1,0:T(8,128)S(1)}, u32[]{:S(2)}, u32[]{:S(2)}) collective-permute-start(f32[112,128]{1,0:T(8,128)S(1)} %get-tuple-element.63), channel_id=1, source_target_pairs={{32,0},{64,32},{96,64},{128,96},{160,128},{192,160},{224,192},{256... | collective-permute-start | bytes 172040 | tf_op jit(solution)/shard_map/ppermute | solution.py:419
  15.9 2.9 %collective-permute-start.2 = (f32[112,128]{1,0:T(8,128)S(1)}, f32[112,128]{1,0:T(8,128)S(1)}, u32[]{:S(2)}, u32[]{:S(2)}) collective-permute-start(f32[112,128]{1,0:T(8,128)S(1)} %get-tuple-element.64), channel_id=1, source_target_pairs={{0,1},{1,2},{2,3},{3,4},{4,5},{5,6},{6,7},{7,8},{8,9},{9,10},{10,1... | collective-permute-start | bytes 172040 | tf_op jit(solution)/shard_map/ppermute | solution.py:419
  18.9 10.4 %collective-permute-start.3 = (f32[112,128]{1,0:T(8,128)S(1)}, f32[112,128]{1,0:T(8,128)S(1)}, u32[]{:S(2)}, u32[]{:S(2)}) collective-permute-start(f32[112,128]{1,0:T(8,128)S(1)} %get-tuple-element.65), channel_id=1, source_target_pairs={{1,0},{2,1},{3,2},{4,3},{5,4},{6,5},{7,6},{8,7},{9,8},{10,9},{11,1... | collective-permute-start | bytes 172040 | tf_op jit(solution)/shard_map/ppermute | solution.py:419
  29.3 0.0 copy-done
  29.3 1.8 %shard_map.146 = (f32[56,1152]{1,0:T(8,128)S(1)}, f32[4,216,128]{2,1,0:T(8,128)S(1)}, f32[296,128]{1,0:T(8,128)S(1)}, f32[56,56]{1,0:T(8,128)S(1)}, f32[56,288]{1,0:T(8,128)S(1)}, /*index=5*/s32[2,128]{1,0:T(2,128)S(1)}) custom-call(f32[9,56,128]{2,1,0:T(8,128)S(1)} %get-tuple-element.46.refs_0_, f32[56,1152]{1,0:T(8,128)S(1)} %get-tuple-element.47.refs_1_, ...), custom_call_target="tpu_custom_call" | custom-call | tf_op jit(solution)/shard_map/pallas_call | solution.py:403
  31.1 0.0 collective-permute-done.refs_2_
  31.1 0.0 collective-permute-done.1.refs_3_
  31.1 0.0 collective-permute-done.2.refs_4_
  31.1 0.0 collective-permute-done.3.refs_5_
  31.1 1.1 %shard_map.147 = (f32[56,1152]{1,0:T(8,128)S(1)}, f32[256,128]{1,0:T(8,128)S(1)}) custom-call(f32[56,1152]{1,0:T(8,128)S(1)} %get-tuple-element.60.refs_0_, f32[4,216,128]{2,1,0:T(8,128)S(1)} %get-tuple-element.61.refs_1_, f32[112,128]{1,0:T(8,128)S(1)} %collective-permute-done.refs_2_, f32[112,128]{1,0:T(8,128)S(1)} %collective-permute-done.1.refs_3_, ...), custom_call_target="tpu_custom_call" | custom-call | tf_op jit(solution)/shard_map/pallas_call | solution.py:403
  32.2 26.4 %all_to_all.11 = f32[32,8,128]{2,1,0:T(8,128)S(1)} all-to-all(f32[32,8,128]{2,1,0:T(8,128)S(1)} %bitcast.20), channel_id=1, replica_groups=mesh['group'=32,'dom'=32] {'dom'}, dimensions={0} | all-to-all | bytes 262144 | tf_op jit(solution)/shard_map/all_to_all | solution.py:488
  58.6 4.6 %shard_map.148 = (f32[56,1152]{1,0:T(8,128)S(1)}, f32[4,216,128]{2,1,0:T(8,128)S(1)}, f32[112,128]{1,0:T(8,128)S(1)}, f32[112,128]{1,0:T(8,128)S(1)}, f32[112,12...) custom-call(f32[56,1152]{1,0:T(8,128)S(1)} %get-tuple-element.70.ref, ...), custom_call_target="tpu_custom_call" | custom-call | tf_op jit(solution)/shard_map/pallas_call | solution.py:403
  63.2 1.9 %collective-permute-start.4 = (f32[112,128]{1,0:T(8,128)S(1)}, f32[112,128]{1,0:T(8,128)S(1)}, u32[]{:S(2)}, u32[]{:S(2)}) collective-permute-start(f32[112,128]{1,0:T(8,128)S(1)} %get-tuple-element.82), channel_id=1, source_target_pairs={{0,32},{32,64},{64,96},{96,128},{128,160},{160,192},{192,224},{224... | collective-permute-start | bytes 172040 | tf_op jit(solution)/shard_map/ppermute | solution.py:419
  65.1 6.7 %collective-permute-start.5 = (f32[112,128]{1,0:T(8,128)S(1)}, f32[112,128]{1,0:T(8,128)S(1)}, u32[]{:S(2)}, u32[]{:S(2)}) collective-permute-start(f32[112,128]{1,0:T(8,128)S(1)} %get-tuple-element.83), channel_id=1, source_target_pairs={{32,0},{64,32},{96,64},{128,96},{160,128},{192,160},{224,192},{256... | collective-permute-start | bytes 172040 | tf_op jit(solution)/shard_map/ppermute | solution.py:419
  71.8 2.1 %collective-permute-start.6 = (f32[112,128]{1,0:T(8,128)S(1)}, f32[112,128]{1,0:T(8,128)S(1)}, u32[]{:S(2)}, u32[]{:S(2)}) collective-permute-start(f32[112,128]{1,0:T(8,128)S(1)} %get-tuple-element.84), channel_id=1, source_target_pairs={{0,1},{1,2},{2,3},{3,4},{4,5},{5,6},{6,7},{7,8},{8,9},{9,10},{10,1... | collective-permute-start | bytes 172040 | tf_op jit(solution)/shard_map/ppermute | solution.py:419
  73.9 0.1 collective-permute-start.7
  74.0 1.4 %shard_map.149 = (f32[56,1152]{1,0:T(8,128)S(1)}, f32[4,216,128]{2,1,0:T(8,128)S(1)}, f32[296,128]{1,0:T(8,128)S(1)}) custom-call(f32[56,1152]{1,0:T(8,128)S(1)} %get-tuple-element.74.refs_0_, f32[56,1152]{1,0:T(8,128)S(1)} %get-tuple-element.75.refs_1_, f32[4,216,128]{2,1,0:T(8,128)S(1)} %get-tuple-element.76.refs_2_, ...), custom_call_target="tpu_custom_call" | custom-call | tf_op jit(solution)/shard_map/pallas_call | solution.py:403
  75.4 0.0 collective-permute-done.4.refs_2_
  75.5 0.0 collective-permute-done.5.refs_3_
  75.5 0.0 collective-permute-done.6.refs_4_
  75.5 2.3 %collective-permute-done.7.refs_5_ = f32[112,128]{1,0:T(8,128)S(1)} collective-permute-done((f32[112,128]{1,0:T(8,128)S(1)}, f32[112,128]{1,0:T(8,128)S(1)}, u32[]{:S(2)}, u32[]{:S(2)}) %collective-permute-start.7) | collective-permute-done | bytes 57376 | tf_op jit(solution)/shard_map/ppermute | solution.py:419
  77.8 1.6 %shard_map.150 = f32[9,56,128]{2,1,0:T(8,128)} custom-call(f32[56,1152]{1,0:T(8,128)S(1)} %get-tuple-element.80.refs_0_, f32[4,216,128]{2,1,0:T(8,128)S(1)} %get-tuple-element.81.refs_1_, f32[112,128]{1,0:T(8,128)S(1)} %collective-permute-done.4.refs_2_, f32[112,128]{1,0:T(8,128)S(1)} %collective-permute-done.5.refs_3_, ...), custom_call_target="tpu_custom_call" | custom-call | tf_op jit(solution)/shard_map/pallas_call | solution.py:403
  (1 shorter events, 0.0 us)
Async XLA Ops:
  0.0 29.3 %copy-start = (f32[8,2,9,9]{3,1,2,0:T(2,128)S(1)}, f32[8,2,9,9]{3,1,2,0:T(2,128)}, u32[]{:S(2)}) copy-start(f32[8,2,9,9]{3,1,2,0:T(2,128)} %param.19) | copy-start | bytes 15556
  5.9 25.2 %collective-permute-start = (f32[112,128]{1,0:T(8,128)S(1)}, f32[112,128]{1,0:T(8,128)S(1)}, u32[]{:S(2)}, u32[]{:S(2)}) collective-permute-start(f32[112,128]{1,0:T(8,128)S(1)} %get-tuple-element.62), channel_id=1, source_target_pairs={{0,32},{32,64},{64,96},{96,128},{128,160},{160,192},{192,224},{224... | collective-permute-start | bytes 172040 | tf_op jit(solution)/shard_map/ppermute | solution.py:419
  9.9 21.2 %collective-permute-start.1 = (f32[112,128]{1,0:T(8,128)S(1)}, f32[112,128]{1,0:T(8,128)S(1)}, u32[]{:S(2)}, u32[]{:S(2)}) collective-permute-start(f32[112,128]{1,0:T(8,128)S(1)} %get-tuple-element.63), channel_id=1, source_target_pairs={{32,0},{64,32},{96,64},{128,96},{160,128},{192,160},{224,192},{256... | collective-permute-start | bytes 172040 | tf_op jit(solution)/shard_map/ppermute | solution.py:419
  15.9 15.2 %collective-permute-start.2 = (f32[112,128]{1,0:T(8,128)S(1)}, f32[112,128]{1,0:T(8,128)S(1)}, u32[]{:S(2)}, u32[]{:S(2)}) collective-permute-start(f32[112,128]{1,0:T(8,128)S(1)} %get-tuple-element.64), channel_id=1, source_target_pairs={{0,1},{1,2},{2,3},{3,4},{4,5},{5,6},{6,7},{7,8},{8,9},{9,10},{10,1... | collective-permute-start | bytes 172040 | tf_op jit(solution)/shard_map/ppermute | solution.py:419
  18.9 12.2 %collective-permute-start.3 = (f32[112,128]{1,0:T(8,128)S(1)}, f32[112,128]{1,0:T(8,128)S(1)}, u32[]{:S(2)}, u32[]{:S(2)}) collective-permute-start(f32[112,128]{1,0:T(8,128)S(1)} %get-tuple-element.65), channel_id=1, source_target_pairs={{1,0},{2,1},{3,2},{4,3},{5,4},{6,5},{7,6},{8,7},{9,8},{10,9},{11,1... | collective-permute-start | bytes 172040 | tf_op jit(solution)/shard_map/ppermute | solution.py:419
  63.2 12.2 %collective-permute-start.4 = (f32[112,128]{1,0:T(8,128)S(1)}, f32[112,128]{1,0:T(8,128)S(1)}, u32[]{:S(2)}, u32[]{:S(2)}) collective-permute-start(f32[112,128]{1,0:T(8,128)S(1)} %get-tuple-element.82), channel_id=1, source_target_pairs={{0,32},{32,64},{64,96},{96,128},{128,160},{160,192},{192,224},{224... | collective-permute-start | bytes 172040 | tf_op jit(solution)/shard_map/ppermute | solution.py:419
  65.1 10.3 %collective-permute-start.5 = (f32[112,128]{1,0:T(8,128)S(1)}, f32[112,128]{1,0:T(8,128)S(1)}, u32[]{:S(2)}, u32[]{:S(2)}) collective-permute-start(f32[112,128]{1,0:T(8,128)S(1)} %get-tuple-element.83), channel_id=1, source_target_pairs={{32,0},{64,32},{96,64},{128,96},{160,128},{192,160},{224,192},{256... | collective-permute-start | bytes 172040 | tf_op jit(solution)/shard_map/ppermute | solution.py:419
  71.8 3.6 %collective-permute-start.6 = (f32[112,128]{1,0:T(8,128)S(1)}, f32[112,128]{1,0:T(8,128)S(1)}, u32[]{:S(2)}, u32[]{:S(2)}) collective-permute-start(f32[112,128]{1,0:T(8,128)S(1)} %get-tuple-element.84), channel_id=1, source_target_pairs={{0,1},{1,2},{2,3},{3,4},{4,5},{5,6},{6,7},{7,8},{8,9},{9,10},{10,1... | collective-permute-start | bytes 172040 | tf_op jit(solution)/shard_map/ppermute | solution.py:419
  73.9 3.9 %collective-permute-start.7 = (f32[112,128]{1,0:T(8,128)S(1)}, f32[112,128]{1,0:T(8,128)S(1)}, u32[]{:S(2)}, u32[]{:S(2)}) collective-permute-start(f32[112,128]{1,0:T(8,128)S(1)} %get-tuple-element.85), channel_id=1, source_target_pairs={{1,0},{2,1},{3,2},{4,3},{5,4},{6,5},{7,6},{8,7},{9,8},{10,9},{11,1... | collective-permute-start | bytes 172040 | tf_op jit(solution)/shard_map/ppermute | solution.py:419

commit v4 on v2

--- a/solution.py
+++ b/solution.py
@@ -144,8 +144,8 @@
         (wide_ref, deriv_ref, padded_ref, geometry_ref, material_ref, sems) = refs[14 + LATER :]
         targets = [geometry_ref, material_ref] + list(held)
         copies = fetch(list(zip(inputs, targets)), sems)
-        for copy in copies[:7]:
-            copy.wait()
+        for n in (0, 1, 3):
+            copies[n].wait()
         desc_ref[...] = jnp.zeros((8, LANES), f32)
         for d in range(3):
             desc_ref[d : d + 1, :] = geometry_ref[d]
@@ -168,9 +168,6 @@
             placed_ref[:, block(f)] = new
         desc = jnp.where(arrives, moved[FIELDS * modes :], desc)
         integral_ref[...] = placed_ref[...]
-    else:
-        for f in range(FIELDS):
-            integral_ref[:, block(f)] = state_ref[f]
 
     hot = one_hot(desc)
     hot_ref[...] = hot
@@ -180,6 +177,12 @@
     scale = jnp.where(row_at < third, desc[0:1], jnp.where(row_at < 2 * third, desc[1:2], desc[2:3]))
     ops_ref[...] = rows * scale
     spread_rows(ops_ref, 0, 27, wide_ref)
+
+    if not place:
+        for n in (2, 4, 5, 6):
+            copies[n].wait()
+        for f in range(FIELDS):
+            integral_ref[:, block(f)] = state_ref[f]
 
     across = jnp.concatenate([jnp.transpose(stiff_ref[d], (1, 0)) for d in range(3)], axis=0)
     stiff = left_matrix(-jnp.transpose(across, (1, 0)))

time: 79.7 us -> 79.6 us (level)
  no operation moved by 1% of the time
where the time goes in v4:
time: 79.6 us; the launch traced here: 79.4 us
  starting transfers between devices  34.2 us (43%)
  blocking collectives  26.4 us (33%)
  Pallas kernels  16.4 us (21%)
  waiting for transfers between devices  2.34 us (3%)
    ppermute x8, starting transfers between devices, exchange(): out += [lax.ppermute(higher, axis, up), lax.ppermute(lower, axis, down)]  34.2 us
    all_to_all x1, blocking collectives, shards(): lax.all_to_all(packed, 'dom', split_axis=0, concat_axis=0, tiled=True)  26.4 us
    pallas_call x6, Pallas kernels, call(): pl.pallas_call(lambda *refs: body(refs), out_shape=outs, in_specs=[pl.Blo...  16.4 us
    ppermute x8, waiting for transfers between devices, exchange(): out += [lax.ppermute(higher, axis, up), lax.ppermute(lower, axis, down)]  2.34 us
  transfers between devices with their start and end apart: 8, of which 1 were waited for; matrix products, arithmetic and copies ran while one was open for 0% of the time, Pallas kernels for 4%

profile of v4, /device:TPU:1, one launch (start us, length us, event | category | flops | bytes accessed | tf_op | source)
XLA Modules:
  0.0 79.4 jit_solution(11397122576226966877)
XLA Ops:
  0.0 0.0 copy-start
  0.0 5.8 %shard_map.145 = (f32[56,1152]{1,0:T(8,128)S(1)}, f32[4,216,128]{2,1,0:T(8,128)S(1)}, f32[112,128]{1,0:T(8,128)S(1)}, f32[112,128]{1,0:T(8,128)S(1)}, f32[112,12...) custom-call(f32[3,1,128]{2,1,0:T(1,128)} %bitcast.26, ...), custom_call_target="tpu_custom_call" | custom-call | tf_op jit(solution)/shard_map/pallas_call | solution.py:417
  5.8 4.0 %collective-permute-start = (f32[112,128]{1,0:T(8,128)S(1)}, f32[112,128]{1,0:T(8,128)S(1)}, u32[]{:S(2)}, u32[]{:S(2)}) collective-permute-start(f32[112,128]{1,0:T(8,128)S(1)} %get-tuple-element.62), channel_id=1, source_target_pairs={{0,32},{32,64},{64,96},{96,128},{128,160},{160,192},{192,224},{224... | collective-permute-start | bytes 172040 | tf_op jit(solution)/shard_map/ppermute | solution.py:433
  9.8 6.0 %collective-permute-start.1 = (f32[112,128]{1,0:T(8,128)S(1)}, f32[112,128]{1,0:T(8,128)S(1)}, u32[]{:S(2)}, u32[]{:S(2)}) collective-permute-start(f32[112,128]{1,0:T(8,128)S(1)} %get-tuple-element.63), channel_id=1, source_target_pairs={{32,0},{64,32},{96,64},{128,96},{160,128},{192,160},{224,192},{256... | collective-permute-start | bytes 172040 | tf_op jit(solution)/shard_map/ppermute | solution.py:433
  15.9 2.9 %collective-permute-start.2 = (f32[112,128]{1,0:T(8,128)S(1)}, f32[112,128]{1,0:T(8,128)S(1)}, u32[]{:S(2)}, u32[]{:S(2)}) collective-permute-start(f32[112,128]{1,0:T(8,128)S(1)} %get-tuple-element.64), channel_id=1, source_target_pairs={{0,1},{1,2},{2,3},{3,4},{4,5},{5,6},{6,7},{7,8},{8,9},{9,10},{10,1... | collective-permute-start | bytes 172040 | tf_op jit(solution)/shard_map/ppermute | solution.py:433
  18.8 10.4 %collective-permute-start.3 = (f32[112,128]{1,0:T(8,128)S(1)}, f32[112,128]{1,0:T(8,128)S(1)}, u32[]{:S(2)}, u32[]{:S(2)}) collective-permute-start(f32[112,128]{1,0:T(8,128)S(1)} %get-tuple-element.65), channel_id=1, source_target_pairs={{1,0},{2,1},{3,2},{4,3},{5,4},{6,5},{7,6},{8,7},{9,8},{10,9},{11,1... | collective-permute-start | bytes 172040 | tf_op jit(solution)/shard_map/ppermute | solution.py:433
  29.2 0.0 copy-done
  29.2 1.8 %shard_map.146 = (f32[56,1152]{1,0:T(8,128)S(1)}, f32[4,216,128]{2,1,0:T(8,128)S(1)}, f32[296,128]{1,0:T(8,128)S(1)}, f32[56,56]{1,0:T(8,128)S(1)}, f32[56,288]{1,0:T(8,128)S(1)}, /*index=5*/s32[2,128]{1,0:T(2,128)S(1)}) custom-call(f32[9,56,128]{2,1,0:T(8,128)S(1)} %get-tuple-element.46.refs_0_, f32[56,1152]{1,0:T(8,128)S(1)} %get-tuple-element.47.refs_1_, ...), custom_call_target="tpu_custom_call" | custom-call | tf_op jit(solution)/shard_map/pallas_call | solution.py:417
  31.0 0.0 collective-permute-done.refs_2_
  31.0 0.0 collective-permute-done.1.refs_3_
  31.0 0.0 collective-permute-done.2.refs_4_
  31.0 0.0 collective-permute-done.3.refs_5_
  31.0 1.1 %shard_map.147 = (f32[56,1152]{1,0:T(8,128)S(1)}, f32[256,128]{1,0:T(8,128)S(1)}) custom-call(f32[56,1152]{1,0:T(8,128)S(1)} %get-tuple-element.60.refs_0_, f32[4,216,128]{2,1,0:T(8,128)S(1)} %get-tuple-element.61.refs_1_, f32[112,128]{1,0:T(8,128)S(1)} %collective-permute-done.refs_2_, f32[112,128]{1,0:T(8,128)S(1)} %collective-permute-done.1.refs_3_, ...), custom_call_target="tpu_custom_call" | custom-call | tf_op jit(solution)/shard_map/pallas_call | solution.py:417
  32.1 26.4 %all_to_all.11 = f32[32,8,128]{2,1,0:T(8,128)S(1)} all-to-all(f32[32,8,128]{2,1,0:T(8,128)S(1)} %bitcast.20), channel_id=1, replica_groups=mesh['group'=32,'dom'=32] {'dom'}, dimensions={0} | all-to-all | bytes 262144 | tf_op jit(solution)/shard_map/all_to_all | solution.py:505
  58.5 4.6 %shard_map.148 = (f32[56,1152]{1,0:T(8,128)S(1)}, f32[4,216,128]{2,1,0:T(8,128)S(1)}, f32[112,128]{1,0:T(8,128)S(1)}, f32[112,128]{1,0:T(8,128)S(1)}, f32[112,12...) custom-call(f32[56,1152]{1,0:T(8,128)S(1)} %get-tuple-element.70.ref, ...), custom_call_target="tpu_custom_call" | custom-call | tf_op jit(solution)/shard_map/pallas_call | solution.py:417
  63.1 1.9 %collective-permute-start.4 = (f32[112,128]{1,0:T(8,128)S(1)}, f32[112,128]{1,0:T(8,128)S(1)}, u32[]{:S(2)}, u32[]{:S(2)}) collective-permute-start(f32[112,128]{1,0:T(8,128)S(1)} %get-tuple-element.82), channel_id=1, source_target_pairs={{0,32},{32,64},{64,96},{96,128},{128,160},{160,192},{192,224},{224... | collective-permute-start | bytes 172040 | tf_op jit(solution)/shard_map/ppermute | solution.py:433
  65.0 6.7 %collective-permute-start.5 = (f32[112,128]{1,0:T(8,128)S(1)}, f32[112,128]{1,0:T(8,128)S(1)}, u32[]{:S(2)}, u32[]{:S(2)}) collective-permute-start(f32[112,128]{1,0:T(8,128)S(1)} %get-tuple-element.83), channel_id=1, source_target_pairs={{32,0},{64,32},{96,64},{128,96},{160,128},{192,160},{224,192},{256... | collective-permute-start | bytes 172040 | tf_op jit(solution)/shard_map/ppermute | solution.py:433
  71.7 2.1 %collective-permute-start.6 = (f32[112,128]{1,0:T(8,128)S(1)}, f32[112,128]{1,0:T(8,128)S(1)}, u32[]{:S(2)}, u32[]{:S(2)}) collective-permute-start(f32[112,128]{1,0:T(8,128)S(1)} %get-tuple-element.84), channel_id=1, source_target_pairs={{0,1},{1,2},{2,3},{3,4},{4,5},{5,6},{6,7},{7,8},{8,9},{9,10},{10,1... | collective-permute-start | bytes 172040 | tf_op jit(solution)/shard_map/ppermute | solution.py:433
  73.8 0.1 collective-permute-start.7
  73.9 1.4 %shard_map.149 = (f32[56,1152]{1,0:T(8,128)S(1)}, f32[4,216,128]{2,1,0:T(8,128)S(1)}, f32[296,128]{1,0:T(8,128)S(1)}) custom-call(f32[56,1152]{1,0:T(8,128)S(1)} %get-tuple-element.74.refs_0_, f32[56,1152]{1,0:T(8,128)S(1)} %get-tuple-element.75.refs_1_, f32[4,216,128]{2,1,0:T(8,128)S(1)} %get-tuple-element.76.refs_2_, ...), custom_call_target="tpu_custom_call" | custom-call | tf_op jit(solution)/shard_map/pallas_call | solution.py:417
  75.4 0.0 collective-permute-done.4.refs_2_
  75.4 0.0 collective-permute-done.5.refs_3_
  75.4 0.0 collective-permute-done.6.refs_4_
  75.4 2.3 %collective-permute-done.7.refs_5_ = f32[112,128]{1,0:T(8,128)S(1)} collective-permute-done((f32[112,128]{1,0:T(8,128)S(1)}, f32[112,128]{1,0:T(8,128)S(1)}, u32[]{:S(2)}, u32[]{:S(2)}) %collective-permute-start.7) | collective-permute-done | bytes 57376 | tf_op jit(solution)/shard_map/ppermute | solution.py:433
  77.7 1.6 %shard_map.150 = f32[9,56,128]{2,1,0:T(8,128)} custom-call(f32[56,1152]{1,0:T(8,128)S(1)} %get-tuple-element.80.refs_0_, f32[4,216,128]{2,1,0:T(8,128)S(1)} %get-tuple-element.81.refs_1_, f32[112,128]{1,0:T(8,128)S(1)} %collective-permute-done.4.refs_2_, f32[112,128]{1,0:T(8,128)S(1)} %collective-permute-done.5.refs_3_, ...), custom_call_target="tpu_custom_call" | custom-call | tf_op jit(solution)/shard_map/pallas_call | solution.py:417
  (1 shorter events, 0.0 us)
Async XLA Ops:
  0.0 29.2 %copy-start = (f32[8,2,9,9]{3,1,2,0:T(2,128)S(1)}, f32[8,2,9,9]{3,1,2,0:T(2,128)}, u32[]{:S(2)}) copy-start(f32[8,2,9,9]{3,1,2,0:T(2,128)} %param.19) | copy-start | bytes 15556
  5.8 25.2 %collective-permute-start = (f32[112,128]{1,0:T(8,128)S(1)}, f32[112,128]{1,0:T(8,128)S(1)}, u32[]{:S(2)}, u32[]{:S(2)}) collective-permute-start(f32[112,128]{1,0:T(8,128)S(1)} %get-tuple-element.62), channel_id=1, source_target_pairs={{0,32},{32,64},{64,96},{96,128},{128,160},{160,192},{192,224},{224... | collective-permute-start | bytes 172040 | tf_op jit(solution)/shard_map/ppermute | solution.py:433
  9.8 21.2 %collective-permute-start.1 = (f32[112,128]{1,0:T(8,128)S(1)}, f32[112,128]{1,0:T(8,128)S(1)}, u32[]{:S(2)}, u32[]{:S(2)}) collective-permute-start(f32[112,128]{1,0:T(8,128)S(1)} %get-tuple-element.63), channel_id=1, source_target_pairs={{32,0},{64,32},{96,64},{128,96},{160,128},{192,160},{224,192},{256... | collective-permute-start | bytes 172040 | tf_op jit(solution)/shard_map/ppermute | solution.py:433
  15.9 15.2 %collective-permute-start.2 = (f32[112,128]{1,0:T(8,128)S(1)}, f32[112,128]{1,0:T(8,128)S(1)}, u32[]{:S(2)}, u32[]{:S(2)}) collective-permute-start(f32[112,128]{1,0:T(8,128)S(1)} %get-tuple-element.64), channel_id=1, source_target_pairs={{0,1},{1,2},{2,3},{3,4},{4,5},{5,6},{6,7},{7,8},{8,9},{9,10},{10,1... | collective-permute-start | bytes 172040 | tf_op jit(solution)/shard_map/ppermute | solution.py:433
  18.8 12.2 %collective-permute-start.3 = (f32[112,128]{1,0:T(8,128)S(1)}, f32[112,128]{1,0:T(8,128)S(1)}, u32[]{:S(2)}, u32[]{:S(2)}) collective-permute-start(f32[112,128]{1,0:T(8,128)S(1)} %get-tuple-element.65), channel_id=1, source_target_pairs={{1,0},{2,1},{3,2},{4,3},{5,4},{6,5},{7,6},{8,7},{9,8},{10,9},{11,1... | collective-permute-start | bytes 172040 | tf_op jit(solution)/shard_map/ppermute | solution.py:433
  63.1 12.3 %collective-permute-start.4 = (f32[112,128]{1,0:T(8,128)S(1)}, f32[112,128]{1,0:T(8,128)S(1)}, u32[]{:S(2)}, u32[]{:S(2)}) collective-permute-start(f32[112,128]{1,0:T(8,128)S(1)} %get-tuple-element.82), channel_id=1, source_target_pairs={{0,32},{32,64},{64,96},{96,128},{128,160},{160,192},{192,224},{224... | collective-permute-start | bytes 172040 | tf_op jit(solution)/shard_map/ppermute | solution.py:433
  65.0 10.3 %collective-permute-start.5 = (f32[112,128]{1,0:T(8,128)S(1)}, f32[112,128]{1,0:T(8,128)S(1)}, u32[]{:S(2)}, u32[]{:S(2)}) collective-permute-start(f32[112,128]{1,0:T(8,128)S(1)} %get-tuple-element.83), channel_id=1, source_target_pairs={{32,0},{64,32},{96,64},{128,96},{160,128},{192,160},{224,192},{256... | collective-permute-start | bytes 172040 | tf_op jit(solution)/shard_map/ppermute | solution.py:433
  71.7 3.7 %collective-permute-start.6 = (f32[112,128]{1,0:T(8,128)S(1)}, f32[112,128]{1,0:T(8,128)S(1)}, u32[]{:S(2)}, u32[]{:S(2)}) collective-permute-start(f32[112,128]{1,0:T(8,128)S(1)} %get-tuple-element.84), channel_id=1, source_target_pairs={{0,1},{1,2},{2,3},{3,4},{4,5},{5,6},{6,7},{7,8},{8,9},{9,10},{10,1... | collective-permute-start | bytes 172040 | tf_op jit(solution)/shard_map/ppermute | solution.py:433
  73.8 3.9 %collective-permute-start.7 = (f32[112,128]{1,0:T(8,128)S(1)}, f32[112,128]{1,0:T(8,128)S(1)}, u32[]{:S(2)}, u32[]{:S(2)}) collective-permute-start(f32[112,128]{1,0:T(8,128)S(1)} %get-tuple-element.85), channel_id=1, source_target_pairs={{1,0},{2,1},{3,2},{4,3},{5,4},{6,5},{7,6},{8,7},{9,8},{10,9},{11,1... | collective-permute-start | bytes 172040 | tf_op jit(solution)/shard_map/ppermute | solution.py:433
